TPU v7x, 128 devices: a whole 4x4x4 slice. The times are simulated.
128 devices in a mesh: tm: 8 (over y_hi, x), freq: 16 (over z, y_lo, core).
Axes of the slice: x: 4, y: 4 (y_hi: 2, y_lo: 2; y = y_hi * 2 + y_lo), z: 4, core: 2. Of those that a mesh axis runs over, the one named last changes fastest.
Arguments:
- voltages: bfloat16 [512, 262144], P('freq', 'tm'), may hold values from -6 to 6
- station_flags: int32 [256], replicated, may hold values 0 or 1
- owner_map: int32 [1024], replicated, may hold values from 0 to 1023, each once
- beam_table: int32 [256], replicated, may hold values from 0 to 255, each once
- table_gains: float32 [256, 512], replicated, may hold values from 0.5 to 2
- table_delays: float32 [256, 512], replicated, may hold values from -8 to 8
Outputs:
- visibilities: bfloat16 [1024, 2, 512, 512], P(('tm', 'freq'))
- beam_voltages: bfloat16 [1024, 128, 2, 256], P(('tm', 'freq'))
Inputs may be any that keep to these rules, and one draw needn't show every extreme that they name: `owner_map`: every channel appears in exactly one slot. `beam_table`: every weight table belongs to exactly one beam.
All inputs are finite; a program needn't handle non-finite values.
Results may differ from a plain program's by a relative error of at most 0.007.
Values may be sent and summed in bfloat16 or wider, within the bound.
No kernel may reach another device: no remote copies, remote signals or barrier semaphores. Data moves between devices by JAX's collectives and lax.ppermute only.
A program may use at most 512 MiB of HBM per device.

v0:
```python
import functools
import math

import jax
import jax.numpy as jnp
import numpy as np
from jax import lax
from jax.experimental import pallas as pl
from jax.experimental.pallas import tpu as pltpu
from jax.sharding import PartitionSpec as P

INPUTS = 512
CH = 1024
L = 2048
TAPS = 16
BEAMS = 256
NTAB = 256
FR = 16
IN_DEV = 32
SLOTS = 8
BF = jnp.bfloat16
F32 = jnp.float32
MIB = 1 << 20
VM = pl.BlockSpec(memory_space=pltpu.VMEM)
SM = pl.BlockSpec(memory_space=pltpu.SMEM)
ANY = pl.BlockSpec(memory_space=pl.ANY)


def fit(fn, degree):
    nodes = np.cos(np.pi * (np.arange(64) + 0.5) / 64) * 0.125 + 0.125
    poly = np.polynomial.Chebyshev.fit(nodes, fn(np.sqrt(nodes)), degree, domain=[0.0, 0.25])
    return [float(c) for c in poly.convert(kind=np.polynomial.Polynomial).coef]


COS = fit(lambda r: np.cos(2 * np.pi * r), 6)
NEG_SIN = fit(lambda r: -np.sin(2 * np.pi * r) / r, 6)


def horner(coefs, z):
    total = z * coefs[-1] + coefs[-2]
    for c in coefs[-3::-1]:
        total = total * z + c
    return total


def cos_negsin(turns):
    r = turns - jnp.floor(turns + 0.5)
    z = r * r
    return horner(COS, z), horner(NEG_SIN, z) * r


def taps_table():
    index = np.arange(TAPS * L).astype(np.float64)
    offset = (index - TAPS * L / 2 + 0.5) / L
    window = 0.5 - 0.5 * np.cos(2.0 * np.pi * (index + 0.5) / (TAPS * L))
    return (np.sinc(offset) * window).reshape(TAPS, L).astype(np.float32)


def lane_order():
    m = np.zeros((512, 512), np.float32)
    for fl in range(4):
        for tl in range(4):
            for i in range(32):
                m[fl * 128 + tl * 32 + i, tl * 128 + fl * 32 + i] = 1
    return m


def frames_of(phase):
    return [4 + u for u in range(8)] if phase == 0 else [0, 1, 2, 3, 12, 13, 14, 15]


def frame_order():
    m = np.zeros((256, 256), np.float32)
    for c in range(2):
        for tl in range(4):
            for tm in range(8):
                for ph in range(2):
                    for th in range(2):
                        o = frames_of(ph)[th * 4 + tl]
                        t = (tm * FR + 8 + o) % 128
                        m[t * 2 + c, c * 128 + tl * 32 + tm * 4 + ph * 2 + th] = 1
    return m


def table_kernel(chan_ref, cos_ref, sin_ref):
    def group(g, carry):
        chan = chan_ref[:, g].reshape(64, 128)
        n2 = lax.broadcasted_iota(jnp.int32, (64, 128), 1).astype(F32)
        c, s = cos_negsin(chan * n2 * (1.0 / L))
        a, b = cos_negsin(chan * (128.0 / L))
        at = pl.ds(pl.multiple_of(g * 64, 64), 64)
        for n1 in range(L // 128):
            cos_ref[at, n1 * 128 : (n1 + 1) * 128] = c.astype(BF)
            sin_ref[at, n1 * 128 : (n1 + 1) * 128] = s.astype(BF)
            if n1 < L // 128 - 1:
                c, s = c * a - s * b, s * a + c * b
        return carry

    lax.fori_loop(0, 16, group, 0)


def make_table(owner_map):
    chan = jnp.broadcast_to(owner_map.astype(F32)[:, None], (CH, 128)).reshape(8, 16, SLOTS, 128)
    return pl.pallas_call(
        table_kernel,
        in_specs=[VM],
        out_specs=[VM, VM],
        out_shape=[pltpu.VMEM((CH, L), BF)] * 2,
        cost_estimate=pl.CostEstimate(flops=16 * CH * L, transcendentals=0, bytes_accessed=8 * MIB),
        compiler_params=pltpu.CompilerParams(vmem_limit_bytes=4 * MIB),
        name="table",
    )(chan)


def weight_kernel(owner_ref, beam_ref, gains_ref, delays_ref, out_ref, gain, delay):
    def pick(g, carry):
        for j in range(8):
            b = g * 8 + j
            row = beam_ref[b]
            gain[pl.ds(b, 1), :] = gains_ref[pl.ds(row, 1), :]
            delay[pl.ds(b, 1), :] = delays_ref[pl.ds(row, 1), :]
        return carry

    lax.fori_loop(0, BEAMS // 8, pick, 0)
    start = (lax.axis_index("tm") * 16 + lax.axis_index("freq")) * SLOTS

    def group(g, carry):
        s = g // (BEAMS // 32)
        at = pl.ds(pl.multiple_of(g % (BEAMS // 32) * 32, 32), 32)
        chan = owner_ref[start + s].astype(F32) * (1.0 / L)
        c, n = cos_negsin(delay[at, :] * chan)
        scaled = gain[at, :] * (1.0 / math.sqrt(INPUTS))
        out_ref[s, 0, at, :] = (scaled * c).astype(BF)
        out_ref[s, 1, at, :] = (scaled * n).astype(BF)
        return carry

    lax.fori_loop(0, SLOTS * BEAMS // 32, group, 0)


def make_weights(owner_map, beam_table, gains, delays):
    return pl.pallas_call(
        weight_kernel,
        in_specs=[SM, SM, VM, VM],
        out_specs=VM,
        out_shape=pltpu.VMEM((SLOTS, 2, BEAMS, INPUTS), BF),
        scratch_shapes=[pltpu.VMEM((BEAMS, INPUTS), F32)] * 2,
        cost_estimate=pl.CostEstimate(flops=50 * SLOTS * INPUTS * BEAMS, transcendentals=0, bytes_accessed=6 * MIB),
        compiler_params=pltpu.CompilerParams(vmem_limit_bytes=4 * MIB),
        name="weights",
    )(owner_map, beam_table, gains, delays)


def spectra_kernel(phase, *refs):
    if phase == 0:
        own, p1, n1, taps_ref, cos_ref, sin_ref, out, filt, message, sem = refs
        p2 = n2 = None
    else:
        own, p1, n1, p2, n2, taps_ref, cos_ref, sin_ref, *_, out, filt, message, sem = refs
    pieces = [(p2, f) for f in range(4)] + [(p1, f) for f in range(3)] + [(own, f) for f in range(FR)]
    pieces += [(n1, f) for f in range(4)] + [(n2, f) for f in range(4)]
    outs = frames_of(phase)
    keep = (lax.axis_index("tm") != lax.axis_size("tm") - 1).astype(F32)

    def column(j, carry):
        at = pl.multiple_of(j * 128, 128)
        taps = [taps_ref[k : k + 1, pl.ds(at, 128)] for k in range(TAPS)]
        for g in range(IN_DEV // 16):
            acc = {}
            for f, (ref, i) in enumerate(pieces):
                hit = [o for o in outs if o <= f < o + TAPS]
                if f == 23:
                    for o in acc:
                        if o >= 8:
                            acc[o] = acc[o] * keep
                if not hit:
                    continue
                x = ref[g * 16 : g * 16 + 16, pl.ds(i * L + at, 128)].astype(F32)
                for o in hit:
                    term = taps[f - o] * x
                    acc[o] = acc[o] + term if o in acc else term
                if f - TAPS + 1 in acc:
                    o = f - TAPS + 1
                    u = outs.index(o) * IN_DEV + g * 16
                    filt[u : u + 16, pl.ds(at, 128)] = acc.pop(o).astype(BF)
        return carry

    lax.fori_loop(0, L // 128, column, 0)
    copies = []
    for q in range(4):
        rows = slice(q * 256, q * 256 + 256)
        dot = lambda ref: lax.dot_general(
            ref[rows, :], filt[...], (((1,), (1,)), ((), ())), preferred_element_type=F32
        ) * (1.0 / math.sqrt(L))
        re, im = dot(cos_ref), dot(sin_ref)
        for th in range(2):
            lanes = slice(th * 128, th * 128 + 128)
            both = [re[:, lanes].reshape(32, SLOTS, 128), im[:, lanes].reshape(32, SLOTS, 128)]
            message[q * 32 : q * 32 + 32, th * 16 : th * 16 + 16, :] = jnp.concatenate(both, 1).astype(BF)
        copy = pltpu.make_async_copy(
            message.at[pl.ds(q * 32, 32)], out.at[pl.ds(q * 32, 32), pl.ds(phase * 32, 32)], sem.at[q]
        )
        copy.start()
        copies.append(copy)
    for copy in copies:
        copy.wait()


def make_spectra(phase, parts, taps, cos, sin, after=(), before=None):
    args = [*parts, taps, cos, sin, *after] + ([] if before is None else [before])
    return pl.pallas_call(
        functools.partial(spectra_kernel, phase),
        in_specs=[VM] * (len(parts) + 3) + [ANY] * (len(args) - len(parts) - 3),
        out_specs=ANY,
        out_shape=jax.ShapeDtypeStruct((128, 64, 128), BF),
        input_output_aliases={} if before is None else {len(args) - 1: 0},
        scratch_shapes=[
            pltpu.VMEM((8 * IN_DEV, L), BF),
            pltpu.VMEM((128, 32, 128), BF),
            pltpu.SemaphoreType.DMA((4,)),
        ],
        cost_estimate=pl.CostEstimate(flops=4 * CH * L * 256, transcendentals=0, bytes_accessed=12 * MIB),
        compiler_params=pltpu.CompilerParams(vmem_limit_bytes=8 * MIB),
        name="spectra%d" % phase,
    )(*args)


def pair_kernel(flag_ref, lanes_ref, frames_ref, got_ref, weight_ref, vis, beam, y, vis_buf, beam_buf, sem, beam_sem):
    dot = functools.partial(jnp.dot, preferred_element_type=F32)
    dot_t = lambda a, b: lax.dot_general(a, b, (((1,), (1,)), ((), ())), preferred_element_type=F32)
    for fh in range(4):
        parts = [got_ref[(fh * 4 + fl) * 8 : (fh * 4 + fl) * 8 + 8].reshape(512, 128) for fl in range(4)]
        block = dot(jnp.concatenate(parts, 1), lanes_ref[...])
        flag = flag_ref[:, fh * 128 : (fh + 1) * 128]
        for tl in range(4):
            y[fh * 4 + tl] = block[:, tl * 128 : (tl + 1) * 128] * flag
    copies = {}
    for s in range(SLOTS):
        b = s % 2
        z = [
            jnp.concatenate(
                [
                    jnp.concatenate([y[fh * 4 + tl, pl.ds(r * 8 + s, 32, stride=16), :] for fh in range(4)], 1)
                    for tl in range(4)
                ],
                0,
            ).astype(BF)
            for r in range(2)
        ]
        w = jnp.concatenate(z, 0)
        wt = w.T
        vt = jnp.concatenate([wt[:, 128:], -wt[:, :128]], 1)
        if s >= 2:
            for copy in copies.pop(s - 2):
                copy.wait()
        started = []
        for c, left in enumerate((wt, vt)):
            vis_buf[b, c] = (dot(left, w) * (1.0 / 128)).astype(BF)
            started.append(pltpu.make_async_copy(vis_buf.at[b, c], vis.at[s, c], sem.at[b, c]))
            started[-1].start()
        w_re, w_im = weight_ref[s, 0], weight_ref[s, 1]
        b_re = dot_t(z[0], w_re) + dot_t(-z[1], w_im)
        b_im = dot_t(z[0], w_im) + dot_t(z[1], w_re)
        both = jnp.concatenate([b_re, b_im], 0).astype(BF)
        beam_buf[b] = dot(frames_ref[...], both).astype(BF).reshape(128, 2, BEAMS)
        started.append(pltpu.make_async_copy(beam_buf.at[b], beam.at[s], beam_sem.at[b]))
        started[-1].start()
        copies[s] = started
    for started in copies.values():
        for copy in started:
            copy.wait()


def make_outputs(flags, got, weights):
    consts = [jnp.asarray(m, BF) for m in (lane_order(), frame_order())]
    return pl.pallas_call(
        pair_kernel,
        in_specs=[VM] * 5,
        out_specs=[ANY, ANY],
        out_shape=[
            jax.ShapeDtypeStruct((SLOTS, 2, INPUTS, INPUTS), BF),
            jax.ShapeDtypeStruct((SLOTS, 128, 2, BEAMS), BF),
        ],
        scratch_shapes=[
            pltpu.VMEM((16, 512, 128), F32),
            pltpu.VMEM((2, 2, INPUTS, INPUTS), BF),
            pltpu.VMEM((2, 128, 2, BEAMS), BF),
            pltpu.SemaphoreType.DMA((2, 2)),
            pltpu.SemaphoreType.DMA((2,)),
        ],
        compiler_params=pltpu.CompilerParams(vmem_limit_bytes=16 * MIB),
        cost_estimate=pl.CostEstimate(flops=5_000_000_000, transcendentals=0, bytes_accessed=16 * MIB),
        name="pairs",
    )(flags, *consts, got, weights)


def shards(voltages, station_flags, owner_map, beam_table, table_gains, table_delays):
    n_time = lax.axis_size("tm")
    up = lambda a, b: lax.ppermute(voltages[:, a * L : b * L], "tm", [(i, i + 1) for i in range(n_time - 1)])
    down = lambda a, b: lax.ppermute(voltages[:, a * L : b * L], "tm", [(i, (i - 1) % n_time) for i in range(n_time)])
    p1, n1 = up(13, 16), down(0, 4)
    p2, n2 = up(9, 13), down(4, 8)
    cos, sin = make_table(owner_map)
    weights = make_weights(owner_map, beam_table, table_gains, table_delays)
    taps = jnp.asarray(taps_table())
    first = make_spectra(0, (voltages, p1, n1), taps, cos, sin)
    flags = jnp.repeat(station_flags, 2).astype(F32).reshape(1, INPUTS)
    spectra = make_spectra(1, (voltages, p1, n1, p2, n2), taps, cos, sin, (weights, flags), first)
    got = lax.all_to_all(spectra, ("freq", "tm"), split_axis=0, concat_axis=0, tiled=True)
    return make_outputs(flags, got, weights)


def solution(mesh):
    in_specs = (P("freq", "tm"), P(), P(), P(), P(), P())
    out_specs = (P(("tm", "freq"), None, None, None), P(("tm", "freq"), None, None, None))
    return jax.shard_map(shards, mesh=mesh, in_specs=in_specs, out_specs=out_specs, check_vma=False)
```

profile of v0, /device:TPU:1, one launch (start us, length us, event | category | flops | bytes accessed | tf_op | source)
XLA Modules:
  0.0 98.2 jit_solution(12188560287679777765)
XLA Ops:
  0.7 2.7 %fusion = (bf16[32,8192]{1,0:T(8,128)(2,1)}, bf16[32,8192]{1,0:T(8,128)(2,1)}, bf16[32,8192]{1,0:T(8,128)(2,1)}) fusion(bf16[32,32768]{1,0:T(8,128)(2,1)} %refs_0_.3), kind=kLoop, calls=%fused_computation | loop fusion | bytes 3145728 | tf_op jit(solution)/shard_map/slice | solution.py:299
  3.4 5.9 %collective-permute-start.1 = (bf16[32,8192]{1,0:T(8,128)(2,1)}, bf16[32,8192]{1,0:T(8,128)(2,1)S(1)}, u32[]{:S(2)}, u32[]{:S(2)}) collective-permute-start(bf16[32,8192]{1,0:T(8,128)(2,1)} %get-tuple-element.8), channel_id=1, source_target_pairs={{0,112},{16,0},{32,16},{48,32},{64,48},{80,64},{96,80},{112,96},{1... | collective-permute-start | bytes 1572872 | tf_op jit(solution)/shard_map/ppermute | solution.py:299
  9.3 0.8 slice.12
  10.1 1.3 %collective-permute-start = (bf16[32,6144]{1,0:T(8,128)(2,1)}, bf16[32,6144]{1,0:T(8,128)(2,1)S(1)}, u32[]{:S(2)}, u32[]{:S(2)}) collective-permute-start(bf16[32,6144]{1,0:T(8,128)(2,1)} %slice.12), channel_id=1, source_target_pairs={{0,16},{16,32},{32,48},{48,64},{64,80},{80,96},{96,112},{1,17},{17... | collective-permute-start | bytes 1179656 | tf_op jit(solution)/shard_map/ppermute | solution.py:298
  11.4 0.6 collective-permute-start.3
  12.0 3.6 %collective-permute-start.2 = (bf16[32,8192]{1,0:T(8,128)(2,1)}, bf16[32,8192]{1,0:T(8,128)(2,1)}, u32[]{:S(2)}, u32[]{:S(2)}) collective-permute-start(bf16[32,8192]{1,0:T(8,128)(2,1)} %get-tuple-element.7), channel_id=1, source_target_pairs={{0,16},{16,32},{32,48},{48,64},{64,80},{80,96},{96,112},{1,17},{17... | collective-permute-start | bytes 1572872 | tf_op jit(solution)/shard_map/ppermute | solution.py:298
  15.6 0.7 broadcast_in_dim.12
  16.4 0.7 broadcast_in_dim.11
  17.1 1.0 %convert_element_type.18.refs_9_.flag_ref = f32[1,512]{1,0:T(1,128)S(1)} reshape(f32[256,2]{1,0:T(8,128)} %broadcast_in_dim.11) | data formatting | bytes 4096 | tf_op jit(solution)/shard_map/convert_element_type | solution.py:306
  18.1 1.0 %broadcast_in_dim.13.chan_ref = f32[8,16,8,128]{3,2,1,0:T(8,128)S(1)} broadcast(f32[8,16,8]{2,1,0:T(8,128)} %broadcast_in_dim.12), dimensions={0,1,2} | broadcast | bytes 528384 | tf_op jit(solution)/shard_map/broadcast_in_dim | solution.py:103
  19.2 3.6 %table.1 = (bf16[1024,2048]{1,0:T(8,128)(2,1)S(1)}, bf16[1024,2048]{1,0:T(8,128)(2,1)S(1)}) custom-call(f32[8,16,8,128]{3,2,1,0:T(8,128)S(1)} %broadcast_in_dim.13.chan_ref), custom_call_target="tpu_custom_call" | custom-call | flops 33554432 | bytes 8388608 | tf_op jit(solution)/shard_map/table/pallas_call | solution.py:104
  22.8 0.0 copy-start.2
  22.8 1.0 %copy-done.2 = f32[256,512]{1,0:T(8,128)S(1)} copy-done((f32[256,512]{1,0:T(8,128)S(1)}, f32[256,512]{1,0:T(8,128)}, u32[]{:S(2)}) %copy-start.2) | copy-done | bytes 524312
  23.8 7.5 %weights.1.refs_8_.weight_ref = bf16[8,2,256,512]{3,2,1,0:T(8,128)(2,1)S(1)} custom-call(s32[1024]{0:T(1024)S(1)} %copy-done.4, s32[256]{0:T(256)S(1)} %copy-done.5, f32[256,512]{1,0:T(8,128)S(1)} %copy-done.1, f32[256,512]{1,0:T(8,128)S(1)} %copy-done.2), custom_call_target="tpu_custom_call" | custom-call | flops 52428800 | bytes 6291456 | tf_op jit(solution)/shard_map/weights/pallas_call | solution.py:141
  31.3 0.0 collective-permute-done.refs_1_
  31.3 0.0 collective-permute-done.1.refs_2_
  31.4 5.9 %spectra0.1.refs_10_ = bf16[128,64,128]{2,1,0:T(8,128)(2,1)S(1)} custom-call(bf16[32,32768]{1,0:T(8,128)(2,1)S(1)} %copy-done, bf16[32,6144]{1,0:T(8,128)(2,1)S(1)} %collective-permute-done.refs_1_, bf16[32,8192]{1,0:T(8,128)(2,1)S(1)} %collective-permute-done.1.refs_2_, f32[16,2048]{1,0:T(8,128)S(1)} %copy-done.3, ...), custom_call_target="tpu_custom_call" | custom-call | flops 2147483648 | bytes 12582912 | tf_op jit(solution)/shard_map/spectra0/pallas_call | solution.py:210
  37.3 0.0 collective-permute-done.3.refs_4_
  37.3 0.0 collective-permute-done.2.refs_3_
  37.3 7.1 %spectra1.1 = bf16[128,64,128]{2,1,0:T(8,128)(2,1)S(1)} custom-call(bf16[32,32768]{1,0:T(8,128)(2,1)S(1)} %copy-done, bf16[32,6144]{1,0:T(8,128)(2,1)S(1)} %collective-permute-done.refs_1_, bf16[32,8192]{1,0:T(8,128)(2,1)S(1)} %collective-permute-done.1.refs_2_, bf16[32,8192]{1,0:T(8,128)(2,1)} %collective-permute-done.2.refs_3_, ...), custom_call_target="tpu_custom_call", output_to_operand_aliasing={{}: (10, {})} | custom-call | flops 2147483648 | bytes 12582912 | tf_op jit(solution)/shard_map/spectra1/pallas_call | solution.py:210
  44.4 0.0 copy-start.6
  44.5 0.0 copy-start.7
  44.5 43.4 %all_to_all.5.got_ref = bf16[128,64,128]{2,1,0:T(8,128)(2,1)S(1)} all-to-all(bf16[128,64,128]{2,1,0:T(8,128)(2,1)S(1)} %spectra1.1), channel_id=1, replica_groups=mesh['tm'=8,'freq'=16] {'freq','tm'}, dimensions={0} | all-to-all | bytes 4194304 | tf_op jit(solution)/shard_map/all_to_all | solution.py:308
  87.9 10.1 %pairs.1 = (bf16[8,2,512,512]{3,2,1,0:T(8,128)(2,1)}, bf16[8,128,2,256]{3,2,1,0:T(2,128)(2,1)}) custom-call(f32[1,512]{1,0:T(1,128)S(1)} %convert_element_type.18.refs_9_.flag_ref, bf16[512,512]{1,0:T(8,128)(2,1)S(1)} %copy-done.6, bf16[256,256]{1,0:T(8,128)(2,1)S(1)} %copy-done.7, bf16[128,64,128]{2,1,0:T(8,128)(2,1)S(1)} %all_to_all.5.got_ref, ...), custom_call_target="tpu_custom_call" | custom-call | flops 5000000000 | bytes 16777216 | tf_op jit(solution)/shard_map/pairs/pallas_call | solution.py:275
  (16 shorter events, 0.0 us)
Async XLA Ops:
  0.6 8.7 %copy-start = (bf16[32,32768]{1,0:T(8,128)(2,1)S(1)}, bf16[32,32768]{1,0:T(8,128)(2,1)}, u32[]{:S(2)}) copy-start(bf16[32,32768]{1,0:T(8,128)(2,1)} %refs_0_.3) | copy-start | bytes 6291460
  0.6 15.0 %copy-start.8 = (s32[256]{0:T(256)S(1)}, s32[256]{0:T(256)}, u32[]{:S(2)}) copy-start(s32[256]{0:T(256)} %param.10) | copy-start | bytes 3076
  0.7 15.0 %copy-start.4 = (s32[1024]{0:T(1024)S(1)}, s32[1024]{0:T(1024)}, u32[]{:S(2)}) copy-start(s32[1024]{0:T(1024)} %owner_ref.1) | copy-start | bytes 12292
  0.7 22.1 %copy-start.1 = (f32[256,512]{1,0:T(8,128)S(1)}, f32[256,512]{1,0:T(8,128)}, u32[]{:S(2)}) copy-start(f32[256,512]{1,0:T(8,128)} %gains_ref.1) | copy-start | bytes 1572868
  0.7 22.1 %copy-start.5 = (s32[256]{0:T(256)S(1)}, s32[256]{0:T(256)}, u32[]{:S(2)}) copy-start(s32[256]{0:T(256)} %beam_ref.1) | copy-start | bytes 3076
  3.4 28.0 %collective-permute-start.1 = (bf16[32,8192]{1,0:T(8,128)(2,1)}, bf16[32,8192]{1,0:T(8,128)(2,1)S(1)}, u32[]{:S(2)}, u32[]{:S(2)}) collective-permute-start(bf16[32,8192]{1,0:T(8,128)(2,1)} %get-tuple-element.8), channel_id=1, source_target_pairs={{0,112},{16,0},{32,16},{48,32},{64,48},{80,64},{96,80},{112,96},{1... | collective-permute-start | bytes 1572872 | tf_op jit(solution)/shard_map/ppermute | solution.py:299
  10.1 21.2 %collective-permute-start = (bf16[32,6144]{1,0:T(8,128)(2,1)}, bf16[32,6144]{1,0:T(8,128)(2,1)S(1)}, u32[]{:S(2)}, u32[]{:S(2)}) collective-permute-start(bf16[32,6144]{1,0:T(8,128)(2,1)} %slice.12), channel_id=1, source_target_pairs={{0,16},{16,32},{32,48},{48,64},{64,80},{80,96},{96,112},{1,17},{17... | collective-permute-start | bytes 1179656 | tf_op jit(solution)/shard_map/ppermute | solution.py:298
  11.4 25.9 %collective-permute-start.3 = (bf16[32,8192]{1,0:T(8,128)(2,1)}, bf16[32,8192]{1,0:T(8,128)(2,1)}, u32[]{:S(2)}, u32[]{:S(2)}) collective-permute-start(bf16[32,8192]{1,0:T(8,128)(2,1)} %get-tuple-element.6), channel_id=1, source_target_pairs={{0,112},{16,0},{32,16},{48,32},{64,48},{80,64},{96,80},{112,96},{1... | collective-permute-start | bytes 1572872 | tf_op jit(solution)/shard_map/ppermute | solution.py:299
  12.0 25.3 %collective-permute-start.2 = (bf16[32,8192]{1,0:T(8,128)(2,1)}, bf16[32,8192]{1,0:T(8,128)(2,1)}, u32[]{:S(2)}, u32[]{:S(2)}) collective-permute-start(bf16[32,8192]{1,0:T(8,128)(2,1)} %get-tuple-element.7), channel_id=1, source_target_pairs={{0,16},{16,32},{32,48},{48,64},{64,80},{80,96},{96,112},{1,17},{17... | collective-permute-start | bytes 1572872 | tf_op jit(solution)/shard_map/ppermute | solution.py:298
  22.8 1.0 %copy-start.2 = (f32[256,512]{1,0:T(8,128)S(1)}, f32[256,512]{1,0:T(8,128)}, u32[]{:S(2)}) copy-start(f32[256,512]{1,0:T(8,128)} %delays_ref.1) | copy-start | bytes 1572868
  23.8 7.5 %copy-start.3 = (f32[16,2048]{1,0:T(8,128)S(1)}, f32[16,2048]{1,0:T(8,128)}, u32[]{:S(2)}) copy-start(f32[16,2048]{1,0:T(8,128)} %constant.6.clone.refs_3_.refs_5_) | copy-start | bytes 393220
  44.4 43.4 %copy-start.6 = (bf16[512,512]{1,0:T(8,128)(2,1)S(1)}, bf16[512,512]{1,0:T(8,128)(2,1)}, u32[]{:S(2)}) copy-start(bf16[512,512]{1,0:T(8,128)(2,1)} %constant.7.clone.lanes_ref) | copy-start | bytes 1572868
  44.5 43.4 %copy-start.7 = (bf16[256,256]{1,0:T(8,128)(2,1)S(1)}, bf16[256,256]{1,0:T(8,128)(2,1)}, u32[]{:S(2)}) copy-start(bf16[256,256]{1,0:T(8,128)(2,1)} %constant.8.clone.frames_ref) | copy-start | bytes 393220
where the time goes:
time: 98.5 us; the launch traced here: 98.2 us
  blocking collectives  43.4 us (44%)
  Pallas kernels  34.2 us (35%)
  starting transfers between devices  11.5 us (12%)
  local copies, waits for them, and re-layouts  8.07 us (8%)
    all_to_all x1, blocking collectives, shards(): lax.all_to_all(spectra, ('freq', 'tm'), split_axis=0, concat_axis=0, tile...  43.4 us
    pallas_call x2, Pallas kernels, make_spectra(): pl.pallas_call(functools.partial(spectra_kernel, phase), in_specs=[VM] *...  13.1 us
    pallas_call x1, Pallas kernels, make_outputs(): pl.pallas_call(pair_kernel, in_specs=[VM] * 5, out_specs=[ANY, ANY], out_...  10.1 us
    pallas_call x1, Pallas kernels, make_weights(): pl.pallas_call(weight_kernel, in_specs=[SM, SM, VM, VM], out_specs=VM, ou...  7.47 us
    ppermute x2, starting transfers between devices, shards(): lax.ppermute(voltages[:, a * L:b * L], 'tm', [(i, (i - 1) % n_time) for i...  6.53 us
    ppermute x2, starting transfers between devices, shards(): lax.ppermute(voltages[:, a * L:b * L], 'tm', [(i, i + 1) for i in range(n...  4.95 us
    pallas_call x1, Pallas kernels, make_table(): pl.pallas_call(table_kernel, in_specs=[VM], out_specs=[VM, VM], out_shape...  3.58 us
    slice x2, local copies, waits for them, and re-layouts, shards(): voltages[:, a * L:b * L]  3.45 us
  transfers between devices with their start and end apart: 4, of which 0 were waited for; matrix products, arithmetic and copies ran while one was open for 4% of the time, Pallas kernels for 17%

commit v1 on v0

--- a/solution.py
+++ b/solution.py
@@ -24,6 +24,7 @@
 VM = pl.BlockSpec(memory_space=pltpu.VMEM)
 SM = pl.BlockSpec(memory_space=pltpu.SMEM)
 ANY = pl.BlockSpec(memory_space=pl.ANY)
+HB = pl.BlockSpec(memory_space=pltpu.HBM)
 
 
 def fit(fn, degree):
@@ -112,7 +113,7 @@
     )(chan)
 
 
-def weight_kernel(owner_ref, beam_ref, gains_ref, delays_ref, out_ref, gain, delay):
+def weight_kernel(owner_ref, beam_ref, gains_ref, delays_ref, out_ref, gain, delay, made, sem):
     def pick(g, carry):
         for j in range(8):
             b = g * 8 + j
@@ -124,64 +125,114 @@
     lax.fori_loop(0, BEAMS // 8, pick, 0)
     start = (lax.axis_index("tm") * 16 + lax.axis_index("freq")) * SLOTS
 
-    def group(g, carry):
-        s = g // (BEAMS // 32)
-        at = pl.ds(pl.multiple_of(g % (BEAMS // 32) * 32, 32), 32)
+    copies = []
+    for s in range(SLOTS):
         chan = owner_ref[start + s].astype(F32) * (1.0 / L)
-        c, n = cos_negsin(delay[at, :] * chan)
-        scaled = gain[at, :] * (1.0 / math.sqrt(INPUTS))
-        out_ref[s, 0, at, :] = (scaled * c).astype(BF)
-        out_ref[s, 1, at, :] = (scaled * n).astype(BF)
-        return carry
-
-    lax.fori_loop(0, SLOTS * BEAMS // 32, group, 0)
+
+        def group(g, carry):
+            at = pl.ds(pl.multiple_of(g * 32, 32), 32)
+            c, n = cos_negsin(delay[at, :] * chan)
+            scaled = gain[at, :] * (1.0 / math.sqrt(INPUTS))
+            made[s, 0, at, :] = (scaled * c).astype(BF)
+            made[s, 1, at, :] = (scaled * n).astype(BF)
+            return carry
+
+        lax.fori_loop(0, BEAMS // 32, group, 0)
+        copies.append(pltpu.make_async_copy(made.at[s], out_ref.at[s], sem.at[s]))
+        copies[-1].start()
+    for copy in copies:
+        copy.wait()
 
 
 def make_weights(owner_map, beam_table, gains, delays):
     return pl.pallas_call(
         weight_kernel,
         in_specs=[SM, SM, VM, VM],
-        out_specs=VM,
-        out_shape=pltpu.VMEM((SLOTS, 2, BEAMS, INPUTS), BF),
-        scratch_shapes=[pltpu.VMEM((BEAMS, INPUTS), F32)] * 2,
+        out_specs=HB,
+        out_shape=pltpu.HBM((SLOTS, 2, BEAMS, INPUTS), BF),
+        scratch_shapes=[
+            pltpu.VMEM((BEAMS, INPUTS), F32),
+            pltpu.VMEM((BEAMS, INPUTS), F32),
+            pltpu.VMEM((SLOTS, 2, BEAMS, INPUTS), BF),
+            pltpu.SemaphoreType.DMA((SLOTS,)),
+        ],
         cost_estimate=pl.CostEstimate(flops=50 * SLOTS * INPUTS * BEAMS, transcendentals=0, bytes_accessed=6 * MIB),
-        compiler_params=pltpu.CompilerParams(vmem_limit_bytes=4 * MIB),
+        compiler_params=pltpu.CompilerParams(vmem_limit_bytes=8 * MIB),
         name="weights",
     )(owner_map, beam_table, gains, delays)
 
 
+def cut_kernel(firsts, source, *refs):
+    outs, sem = refs[:-1], refs[-1]
+    copies = [
+        pltpu.make_async_copy(source.at[:, pl.ds(first * L, out.shape[1])], out, sem.at[i])
+        for i, (first, out) in enumerate(zip(firsts, outs))
+    ]
+    for copy in copies:
+        copy.start()
+    for copy in copies:
+        copy.wait()
+
+
+def cut(voltages, ranges, name):
+    return pl.pallas_call(
+        functools.partial(cut_kernel, [a for a, _ in ranges]),
+        in_specs=[HB],
+        out_specs=[ANY] * len(ranges),
+        out_shape=[jax.ShapeDtypeStruct((IN_DEV, (b - a) * L), BF) for a, b in ranges],
+        scratch_shapes=[pltpu.SemaphoreType.DMA((len(ranges),))],
+        compiler_params=pltpu.CompilerParams(vmem_limit_bytes=MIB),
+        cost_estimate=pl.CostEstimate(flops=0, transcendentals=0, bytes_accessed=2 * MIB),
+        name=name,
+    )(pltpu.with_memory_space_constraint(voltages, pltpu.HBM))
+
+
 def spectra_kernel(phase, *refs):
     if phase == 0:
-        own, p1, n1, taps_ref, cos_ref, sin_ref, out, filt, message, sem = refs
+        own, p1, n1, taps_ref, cos_ref, sin_ref, out, held, filt, message, sem = refs
         p2 = n2 = None
     else:
-        own, p1, n1, p2, n2, taps_ref, cos_ref, sin_ref, *_, out, filt, message, sem = refs
+        p2, n2, taps_ref, cos_ref, sin_ref, held, _, out, filt, message, sem = refs
+        own = p1 = n1 = None
     pieces = [(p2, f) for f in range(4)] + [(p1, f) for f in range(3)] + [(own, f) for f in range(FR)]
     pieces += [(n1, f) for f in range(4)] + [(n2, f) for f in range(4)]
-    outs = frames_of(phase)
-    keep = (lax.axis_index("tm") != lax.axis_size("tm") - 1).astype(F32)
+    now = frames_of(phase)
+    later = frames_of(1)
+    wanted = now + later if phase == 0 else now
+    tm = lax.axis_index("tm")
+    after_first = (tm != 0).astype(F32)
+    before_last = (tm != lax.axis_size("tm") - 1).astype(F32)
 
     def column(j, carry):
         at = pl.multiple_of(j * 128, 128)
-        taps = [taps_ref[k : k + 1, pl.ds(at, 128)] for k in range(TAPS)]
+        lanes = pl.ds(at, 128)
+        taps = [taps_ref[k : k + 1, lanes] for k in range(TAPS)]
         for g in range(IN_DEV // 16):
+            rows = lambda o, among: slice(among.index(o) * IN_DEV + g * 16, among.index(o) * IN_DEV + g * 16 + 16)
             acc = {}
             for f, (ref, i) in enumerate(pieces):
-                hit = [o for o in outs if o <= f < o + TAPS]
-                if f == 23:
+                if f == 7:
+                    for o in acc:
+                        acc[o] = acc[o] * after_first
+                    if phase == 1:
+                        for o in now:
+                            held_o = held[rows(o, later), lanes]
+                            acc[o] = acc[o] + held_o if o in acc else held_o
+                if f == 23 and phase == 0:
                     for o in acc:
                         if o >= 8:
-                            acc[o] = acc[o] * keep
-                if not hit:
-                    continue
-                x = ref[g * 16 : g * 16 + 16, pl.ds(i * L + at, 128)].astype(F32)
+                            acc[o] = acc[o] * before_last
+                hit = [o for o in wanted if o <= f < o + TAPS]
+                if ref is not None and hit:
+                    x = ref[g * 16 : g * 16 + 16, pl.ds(i * L + at, 128)].astype(F32)
+                    for o in hit:
+                        term = taps[f - o] * x
+                        acc[o] = acc[o] + term if o in acc else term
                 for o in hit:
-                    term = taps[f - o] * x
-                    acc[o] = acc[o] + term if o in acc else term
-                if f - TAPS + 1 in acc:
-                    o = f - TAPS + 1
-                    u = outs.index(o) * IN_DEV + g * 16
-                    filt[u : u + 16, pl.ds(at, 128)] = acc.pop(o).astype(BF)
+                    if o == f - TAPS + 1 and o in now:
+                        filt[rows(o, now), lanes] = acc.pop(o).astype(BF)
+                    elif o in later and phase == 0 and f == min(o + TAPS - 1, 26):
+                        held[rows(o, later), lanes] = acc.pop(o)
         return carry
 
     lax.fori_loop(0, L // 128, column, 0)
@@ -196,37 +247,41 @@
             lanes = slice(th * 128, th * 128 + 128)
             both = [re[:, lanes].reshape(32, SLOTS, 128), im[:, lanes].reshape(32, SLOTS, 128)]
             message[q * 32 : q * 32 + 32, th * 16 : th * 16 + 16, :] = jnp.concatenate(both, 1).astype(BF)
-        copy = pltpu.make_async_copy(
-            message.at[pl.ds(q * 32, 32)], out.at[pl.ds(q * 32, 32), pl.ds(phase * 32, 32)], sem.at[q]
-        )
-        copy.start()
-        copies.append(copy)
+        at = pl.ds(q * 32, 32)
+        copies.append(pltpu.make_async_copy(message.at[at], out.at[at, pl.ds(phase * 32, 32)], sem.at[q]))
+        copies[-1].start()
     for copy in copies:
         copy.wait()
 
 
-def make_spectra(phase, parts, taps, cos, sin, after=(), before=None):
-    args = [*parts, taps, cos, sin, *after] + ([] if before is None else [before])
+def make_spectra(phase, args, before=None):
+    args = [*args] + ([] if before is None else [before])
+    out = pltpu.HBM((128, 64, 128), BF)
     return pl.pallas_call(
         functools.partial(spectra_kernel, phase),
-        in_specs=[VM] * (len(parts) + 3) + [ANY] * (len(args) - len(parts) - 3),
-        out_specs=ANY,
-        out_shape=jax.ShapeDtypeStruct((128, 64, 128), BF),
-        input_output_aliases={} if before is None else {len(args) - 1: 0},
+        in_specs=[VM] * (len(args) - 1) + [HB if phase else VM],
+        out_specs=HB if phase else [HB, VM],
+        out_shape=out if phase else [out, pltpu.VMEM((8 * IN_DEV, L), F32)],
+        input_output_aliases={len(args) - 1: 0} if phase else {},
         scratch_shapes=[
             pltpu.VMEM((8 * IN_DEV, L), BF),
             pltpu.VMEM((128, 32, 128), BF),
             pltpu.SemaphoreType.DMA((4,)),
         ],
+        compiler_params=pltpu.CompilerParams(vmem_limit_bytes=8 * MIB),
         cost_estimate=pl.CostEstimate(flops=4 * CH * L * 256, transcendentals=0, bytes_accessed=12 * MIB),
-        compiler_params=pltpu.CompilerParams(vmem_limit_bytes=8 * MIB),
         name="spectra%d" % phase,
     )(*args)
 
 
-def pair_kernel(flag_ref, lanes_ref, frames_ref, got_ref, weight_ref, vis, beam, y, vis_buf, beam_buf, sem, beam_sem):
+def pair_kernel(
+    flag_ref, lanes_ref, frames_ref, got_ref, weights, vis, beam, y, vis_buf, beam_buf, weight_ref, sem, beam_sem, weight_sem
+):
     dot = functools.partial(jnp.dot, preferred_element_type=F32)
     dot_t = lambda a, b: lax.dot_general(a, b, (((1,), (1,)), ((), ())), preferred_element_type=F32)
+    fetches = [pltpu.make_async_copy(weights.at[s], weight_ref.at[s], weight_sem.at[s]) for s in range(SLOTS)]
+    for fetch in fetches:
+        fetch.start()
     for fh in range(4):
         parts = [got_ref[(fh * 4 + fl) * 8 : (fh * 4 + fl) * 8 + 8].reshape(512, 128) for fl in range(4)]
         block = dot(jnp.concatenate(parts, 1), lanes_ref[...])
@@ -235,7 +290,7 @@
             y[fh * 4 + tl] = block[:, tl * 128 : (tl + 1) * 128] * flag
     copies = {}
     for s in range(SLOTS):
-        b = s % 2
+        b = s
         z = [
             jnp.concatenate(
                 [
@@ -249,14 +304,12 @@
         w = jnp.concatenate(z, 0)
         wt = w.T
         vt = jnp.concatenate([wt[:, 128:], -wt[:, :128]], 1)
-        if s >= 2:
-            for copy in copies.pop(s - 2):
-                copy.wait()
         started = []
         for c, left in enumerate((wt, vt)):
             vis_buf[b, c] = (dot(left, w) * (1.0 / 128)).astype(BF)
             started.append(pltpu.make_async_copy(vis_buf.at[b, c], vis.at[s, c], sem.at[b, c]))
             started[-1].start()
+        fetches[s].wait()
         w_re, w_im = weight_ref[s, 0], weight_ref[s, 1]
         b_re = dot_t(z[0], w_re) + dot_t(-z[1], w_im)
         b_im = dot_t(z[0], w_im) + dot_t(z[1], w_re)
@@ -274,7 +327,7 @@
     consts = [jnp.asarray(m, BF) for m in (lane_order(), frame_order())]
     return pl.pallas_call(
         pair_kernel,
-        in_specs=[VM] * 5,
+        in_specs=[VM] * 4 + [HB],
         out_specs=[ANY, ANY],
         out_shape=[
             jax.ShapeDtypeStruct((SLOTS, 2, INPUTS, INPUTS), BF),
@@ -282,29 +335,33 @@
         ],
         scratch_shapes=[
             pltpu.VMEM((16, 512, 128), F32),
-            pltpu.VMEM((2, 2, INPUTS, INPUTS), BF),
-            pltpu.VMEM((2, 128, 2, BEAMS), BF),
-            pltpu.SemaphoreType.DMA((2, 2)),
-            pltpu.SemaphoreType.DMA((2,)),
+            pltpu.VMEM((SLOTS, 2, INPUTS, INPUTS), BF),
+            pltpu.VMEM((SLOTS, 128, 2, BEAMS), BF),
+            pltpu.VMEM((SLOTS, 2, BEAMS, INPUTS), BF),
+            pltpu.SemaphoreType.DMA((SLOTS, 2)),
+            pltpu.SemaphoreType.DMA((SLOTS,)),
+            pltpu.SemaphoreType.DMA((SLOTS,)),
         ],
-        compiler_params=pltpu.CompilerParams(vmem_limit_bytes=16 * MIB),
+        compiler_params=pltpu.CompilerParams(vmem_limit_bytes=24 * MIB),
         cost_estimate=pl.CostEstimate(flops=5_000_000_000, transcendentals=0, bytes_accessed=16 * MIB),
         name="pairs",
-    )(flags, *consts, got, weights)
+    )(flags, *consts, got, pltpu.with_memory_space_constraint(weights, pltpu.HBM))
 
 
 def shards(voltages, station_flags, owner_map, beam_table, table_gains, table_delays):
     n_time = lax.axis_size("tm")
-    up = lambda a, b: lax.ppermute(voltages[:, a * L : b * L], "tm", [(i, i + 1) for i in range(n_time - 1)])
-    down = lambda a, b: lax.ppermute(voltages[:, a * L : b * L], "tm", [(i, (i - 1) % n_time) for i in range(n_time)])
-    p1, n1 = up(13, 16), down(0, 4)
-    p2, n2 = up(9, 13), down(4, 8)
+    up = lambda x: lax.ppermute(x, "tm", [(i, (i + 1) % n_time) for i in range(n_time)])
+    down = lambda x: lax.ppermute(x, "tm", [(i, (i - 1) % n_time) for i in range(n_time)])
+    to_down, to_up = cut(voltages, [(0, 4), (13, 16)], "cut0")
+    n1, p1 = down(to_down), up(to_up)
+    to_down, to_up = cut(voltages, [(4, 8), (9, 13)], "cut1")
+    n2, p2 = down(to_down), up(to_up)
     cos, sin = make_table(owner_map)
+    taps = jnp.asarray(taps_table())
+    first, held = make_spectra(0, (voltages, p1, n1, taps, cos, sin))
+    spectra = make_spectra(1, (p2, n2, taps, cos, sin, held), first)
     weights = make_weights(owner_map, beam_table, table_gains, table_delays)
-    taps = jnp.asarray(taps_table())
-    first = make_spectra(0, (voltages, p1, n1), taps, cos, sin)
     flags = jnp.repeat(station_flags, 2).astype(F32).reshape(1, INPUTS)
-    spectra = make_spectra(1, (voltages, p1, n1, p2, n2), taps, cos, sin, (weights, flags), first)
     got = lax.all_to_all(spectra, ("freq", "tm"), split_axis=0, concat_axis=0, tiled=True)
     return make_outputs(flags, got, weights)
 

time: 98.5 us -> 144 us (1.46)
  Pallas kernels: 34.2 us -> 97.2 us
  blocking collectives: 43.4 us -> 0 us
  waiting for transfers between devices: 0.01 us -> 22.1 us
  starting transfers between devices: 11.5 us -> 21.5 us
  local copies, waits for them, and re-layouts: 8.07 us -> 1.6 us
    pallas_call x2 -> x4, Pallas kernels: 17.6 us -> 80.1 us  [the longest x2 61.8 us: cut(): pl.pallas_call(functools.partial(cut_kernel, [a for a, _ in ranges]), in_...]
    all_to_all x1 -> x0, blocking collectives: 43.4 us -> none  [shards(): lax.all_to_all(spectra, ('freq', 'tm'), split_axis=0, concat_axis=0, tile...]
    all_to_all x0 -> x1, waiting for transfers between devices: none -> 22.1 us  [shards(): lax.all_to_all(spectra, ('freq', 'tm'), split_axis=0, concat_axis=0, tile...]
    all_to_all x0 -> x1, starting transfers between devices: none -> 10.3 us  [shards(): lax.all_to_all(spectra, ('freq', 'tm'), split_axis=0, concat_axis=0, tile...]
    slice x2 -> x0, local copies, waits for them, and re-layouts: 3.45 us -> none  [shards(): voltages[:, a * L:b * L]]
    broadcast_in_dim x2, local copies, waits for them, and re-layouts: 1.75 us -> 0.28 us  [make_table(): jnp.broadcast_to(owner_map.astype(F32)[:, None], (CH, 128))]
  transfers between devices with their start and end apart: 4 -> 5, of which waited for: 0 -> 1; matrix products, arithmetic and copies ran while one was open for 4% -> 0% of each run, Pallas kernels for 17% -> 37%
where the time goes in v1:
time: 144 us; the launch traced here: 143 us
  Pallas kernels  97.2 us (68%)
  waiting for transfers between devices  22.1 us (15%)
  starting transfers between devices  21.5 us (15%)
  local copies, waits for them, and re-layouts  1.6 us (1%)
    pallas_call x2, Pallas kernels, cut(): pl.pallas_call(functools.partial(cut_kernel, [a for a, _ in ranges]), in_...  61.8 us
    all_to_all x1, waiting for transfers between devices, shards(): lax.all_to_all(spectra, ('freq', 'tm'), split_axis=0, concat_axis=0, tile...  22.1 us
    pallas_call x2, Pallas kernels, make_spectra(): pl.pallas_call(functools.partial(spectra_kernel, phase), in_specs=[VM] *...  13.5 us
    ppermute x2, starting transfers between devices, shards(): lax.ppermute(x, 'tm', [(i, (i - 1) % n_time) for i in range(n_time)])  11.2 us
    pallas_call x1, Pallas kernels, make_outputs(): pl.pallas_call(pair_kernel, in_specs=[VM] * 4 + [HB], out_specs=[ANY, ANY...  10.4 us
    all_to_all x1, starting transfers between devices, shards(): lax.all_to_all(spectra, ('freq', 'tm'), split_axis=0, concat_axis=0, tile...  10.3 us
    pallas_call x1, Pallas kernels, make_weights(): pl.pallas_call(weight_kernel, in_specs=[SM, SM, VM, VM], out_specs=HB, ou...  7.88 us
    pallas_call x1, Pallas kernels, make_table(): pl.pallas_call(table_kernel, in_specs=[VM], out_specs=[VM, VM], out_shape...  3.58 us
  transfers between devices with their start and end apart: 5, of which 1 were waited for; matrix products, arithmetic and copies ran while one was open for 0% of the time, Pallas kernels for 37%

profile of v1, /device:TPU:1, one launch (start us, length us, event | category | flops | bytes accessed | tf_op | source)
XLA Modules:
  0.0 143.5 jit_solution(185555985427411573)
XLA Ops:
  0.6 28.9 %cut0.1 = (bf16[32,8192]{1,0:T(8,128)(2,1)}, bf16[32,6144]{1,0:T(8,128)(2,1)}) custom-call(bf16[32,32768]{1,0:T(8,128)(2,1)} %refs_0_.1), custom_call_target="tpu_custom_call" | custom-call | bytes 2097152 | tf_op jit(solution)/shard_map/cut0/pallas_call | solution.py:178
  29.6 0.0 copy-start
  29.6 0.0 copy-start.1
  29.6 6.0 %collective-permute-start.3 = (bf16[32,8192]{1,0:T(8,128)(2,1)}, bf16[32,8192]{1,0:T(8,128)(2,1)S(1)}, u32[]{:S(2)}, u32[]{:S(2)}) collective-permute-start(bf16[32,8192]{1,0:T(8,128)(2,1)} %get-tuple-element.15), channel_id=1, source_target_pairs={{0,112},{16,0},{32,16},{48,32},{64,48},{80,64},{96,80},{112,96},{1... | collective-permute-start | bytes 1572872 | tf_op jit(solution)/shard_map/ppermute | solution.py:354
  35.6 32.9 %cut1.1 = (bf16[32,8192]{1,0:T(8,128)(2,1)}, bf16[32,8192]{1,0:T(8,128)(2,1)}) custom-call(bf16[32,32768]{1,0:T(8,128)(2,1)} %refs_0_.1), custom_call_target="tpu_custom_call" | custom-call | bytes 2097152 | tf_op jit(solution)/shard_map/cut1/pallas_call | solution.py:178
  68.5 0.1 collective-permute-start
  68.6 5.1 %collective-permute-start.1 = (bf16[32,8192]{1,0:T(8,128)(2,1)}, bf16[32,8192]{1,0:T(8,128)(2,1)}, u32[]{:S(2)}, u32[]{:S(2)}) collective-permute-start(bf16[32,8192]{1,0:T(8,128)(2,1)} %get-tuple-element.11), channel_id=1, source_target_pairs={{0,112},{16,0},{32,16},{48,32},{64,48},{80,64},{96,80},{112,96},{1... | collective-permute-start | bytes 1572872 | tf_op jit(solution)/shard_map/ppermute | solution.py:354
  73.7 0.1 broadcast_in_dim.12
  73.8 0.2 broadcast_in_dim.13.chan_ref
  74.0 3.6 %table.1 = (bf16[1024,2048]{1,0:T(8,128)(2,1)S(1)}, bf16[1024,2048]{1,0:T(8,128)(2,1)S(1)}) custom-call(f32[8,16,8,128]{3,2,1,0:T(8,128)S(1)} %broadcast_in_dim.13.chan_ref), custom_call_target="tpu_custom_call" | custom-call | flops 33554432 | bytes 8388608 | tf_op jit(solution)/shard_map/table/pallas_call | solution.py:105
  77.6 8.6 %spectra0.1 = (bf16[128,64,128]{2,1,0:T(8,128)(2,1)}, f32[256,2048]{1,0:T(8,128)S(1)}) custom-call(bf16[32,32768]{1,0:T(8,128)(2,1)S(1)} %copy-done, bf16[32,6144]{1,0:T(8,128)(2,1)} %collective-permute-done.2.refs_1_, bf16[32,8192]{1,0:T(8,128)(2,1)S(1)} %collective-permute-done.3.refs_2_, f32[16,2048]{1,0:T(8,128)S(1)} %copy-done.1, ...), custom_call_target="tpu_custom_call" | custom-call | flops 2147483648 | bytes 12582912 | tf_op jit(solution)/shard_map/spectra0/pallas_call | solution.py:260
  86.3 4.9 %spectra1.1 = bf16[128,64,128]{2,1,0:T(8,128)(2,1)} custom-call(bf16[32,8192]{1,0:T(8,128)(2,1)S(1)} %collective-permute-done.refs_0_, bf16[32,8192]{1,0:T(8,128)(2,1)} %collective-permute-done.1.refs_1_, f32[16,2048]{1,0:T(8,128)S(1)} %copy-done.1, bf16[1024,2048]{1,0:T(8,128)(2,1)S(1)} %get-tuple-element.12.refs_4_.refs_3_, ...), custom_call_target="tpu_custom_call", output_to_operand_aliasing={{}: (6, {})} | custom-call | flops 2147483648 | bytes 12582912 | tf_op jit(solution)/shard_map/spectra1/pallas_call | solution.py:260
  91.2 0.0 copy-start.8
  91.2 0.0 copy-start.2
  91.2 0.0 copy-start.3
  91.2 0.0 copy-start.5
  91.2 10.3 %all-to-all-start = ((bf16[128,64,128]{2,1,0:T(8,128)(2,1)}), bf16[128,64,128]{2,1,0:T(8,128)(2,1)S(1)}, u32[]{:S(2)}, u32[]{:S(2)}) async-start(bf16[128,64,128]{2,1,0:T(8,128)(2,1)} %spectra1.1), calls=%async_computation | async-start | bytes 4194304 | tf_op jit(solution)/shard_map/all_to_all | solution.py:365
  101.5 0.1 broadcast_in_dim.11
  101.6 0.1 convert_element_type.18.flag_ref
  101.8 0.0 copy-start.7
  101.8 7.9 %weights.1 = bf16[8,2,256,512]{3,2,1,0:T(8,128)(2,1)} custom-call(s32[1024]{0:T(1024)S(1)} %copy-done.4, s32[256]{0:T(256)S(1)} %copy-done.5, f32[256,512]{1,0:T(8,128)S(1)} %copy-done.2, f32[256,512]{1,0:T(8,128)S(1)} %copy-done.3), custom_call_target="tpu_custom_call" | custom-call | flops 52428800 | bytes 6291456 | tf_op jit(solution)/shard_map/weights/pallas_call | solution.py:148
  109.7 22.1 %all-to-all-done.got_ref = bf16[128,64,128]{2,1,0:T(8,128)(2,1)S(1)} async-done(((bf16[128,64,128]{2,1,0:T(8,128)(2,1)}), bf16[128,64,128]{2,1,0:T(8,128)(2,1)S(1)}, u32[]{:S(2)}, u32[]{:S(2)}) %all-to-all-start) | async-done | bytes 2097184 | tf_op jit(solution)/shard_map/all_to_all | solution.py:365
  131.8 1.0 copy-done.6
  132.9 10.4 %pairs.1 = (bf16[8,2,512,512]{3,2,1,0:T(8,128)(2,1)}, bf16[8,128,2,256]{3,2,1,0:T(2,128)(2,1)}) custom-call(f32[1,512]{1,0:T(1,128)S(1)} %convert_element_type.18.flag_ref, bf16[512,512]{1,0:T(8,128)(2,1)S(1)} %copy-done.6, bf16[256,256]{1,0:T(8,128)(2,1)S(1)} %copy-done.7, bf16[128,64,128]{2,1,0:T(8,128)(2,1)S(1)} %all-to-all-done.got_ref, ...), custom_call_target="tpu_custom_call" | custom-call | flops 5000000000 | bytes 16777216 | tf_op jit(solution)/shard_map/pairs/pallas_call | solution.py:328
  (17 shorter events, 0.0 us)
Async XLA Ops:
  0.6 73.1 %copy-start.4 = (s32[1024]{0:T(1024)S(1)}, s32[1024]{0:T(1024)}, u32[]{:S(2)}) copy-start(s32[1024]{0:T(1024)} %owner_ref.1) | copy-start | bytes 12292
  29.6 48.1 %copy-start = (bf16[32,32768]{1,0:T(8,128)(2,1)S(1)}, bf16[32,32768]{1,0:T(8,128)(2,1)}, u32[]{:S(2)}) copy-start(bf16[32,32768]{1,0:T(8,128)(2,1)} %refs_0_.1) | copy-start | bytes 6291460
  29.6 48.1 %copy-start.1 = (f32[16,2048]{1,0:T(8,128)S(1)}, f32[16,2048]{1,0:T(8,128)}, u32[]{:S(2)}) copy-start(f32[16,2048]{1,0:T(8,128)} %constant.6.clone.refs_3_.refs_2_) | copy-start | bytes 393220
  29.6 48.0 %collective-permute-start.3 = (bf16[32,8192]{1,0:T(8,128)(2,1)}, bf16[32,8192]{1,0:T(8,128)(2,1)S(1)}, u32[]{:S(2)}, u32[]{:S(2)}) collective-permute-start(bf16[32,8192]{1,0:T(8,128)(2,1)} %get-tuple-element.15), channel_id=1, source_target_pairs={{0,112},{16,0},{32,16},{48,32},{64,48},{80,64},{96,80},{112,96},{1... | collective-permute-start | bytes 1572872 | tf_op jit(solution)/shard_map/ppermute | solution.py:354
  35.6 42.0 %collective-permute-start.2 = (bf16[32,6144]{1,0:T(8,128)(2,1)}, bf16[32,6144]{1,0:T(8,128)(2,1)}, u32[]{:S(2)}, u32[]{:S(2)}) collective-permute-start(bf16[32,6144]{1,0:T(8,128)(2,1)} %get-tuple-element.14), channel_id=1, source_target_pairs={{0,16},{16,32},{32,48},{48,64},{64,80},{80,96},{96,112},{112,0},{1... | collective-permute-start | bytes 1179656 | tf_op jit(solution)/shard_map/ppermute | solution.py:353
  68.5 17.8 %collective-permute-start = (bf16[32,8192]{1,0:T(8,128)(2,1)}, bf16[32,8192]{1,0:T(8,128)(2,1)S(1)}, u32[]{:S(2)}, u32[]{:S(2)}) collective-permute-start(bf16[32,8192]{1,0:T(8,128)(2,1)} %get-tuple-element.10), channel_id=1, source_target_pairs={{0,16},{16,32},{32,48},{48,64},{64,80},{80,96},{96,112},{112,0},{1... | collective-permute-start | bytes 1572872 | tf_op jit(solution)/shard_map/ppermute | solution.py:353
  68.6 17.7 %collective-permute-start.1 = (bf16[32,8192]{1,0:T(8,128)(2,1)}, bf16[32,8192]{1,0:T(8,128)(2,1)}, u32[]{:S(2)}, u32[]{:S(2)}) collective-permute-start(bf16[32,8192]{1,0:T(8,128)(2,1)} %get-tuple-element.11), channel_id=1, source_target_pairs={{0,112},{16,0},{32,16},{48,32},{64,48},{80,64},{96,80},{112,96},{1... | collective-permute-start | bytes 1572872 | tf_op jit(solution)/shard_map/ppermute | solution.py:354
  91.2 10.4 %copy-start.8 = (s32[256]{0:T(256)S(1)}, s32[256]{0:T(256)}, u32[]{:S(2)}) copy-start(s32[256]{0:T(256)} %param.10) | copy-start | bytes 3076
  91.2 10.6 %copy-start.2 = (f32[256,512]{1,0:T(8,128)S(1)}, f32[256,512]{1,0:T(8,128)}, u32[]{:S(2)}) copy-start(f32[256,512]{1,0:T(8,128)} %gains_ref.1) | copy-start | bytes 1572868
  91.2 10.6 %copy-start.3 = (f32[256,512]{1,0:T(8,128)S(1)}, f32[256,512]{1,0:T(8,128)}, u32[]{:S(2)}) copy-start(f32[256,512]{1,0:T(8,128)} %delays_ref.1) | copy-start | bytes 1572868
  91.2 10.6 %copy-start.5 = (s32[256]{0:T(256)S(1)}, s32[256]{0:T(256)}, u32[]{:S(2)}) copy-start(s32[256]{0:T(256)} %beam_ref.1) | copy-start | bytes 3076
  91.2 40.6 %all-to-all-start = ((bf16[128,64,128]{2,1,0:T(8,128)(2,1)}), bf16[128,64,128]{2,1,0:T(8,128)(2,1)S(1)}, u32[]{:S(2)}, u32[]{:S(2)}) async-start(bf16[128,64,128]{2,1,0:T(8,128)(2,1)} %spectra1.1), calls=%async_computation | async-start | bytes 4194304 | tf_op jit(solution)/shard_map/all_to_all | solution.py:365
  101.8 30.0 %copy-start.7 = (bf16[256,256]{1,0:T(8,128)(2,1)S(1)}, bf16[256,256]{1,0:T(8,128)(2,1)}, u32[]{:S(2)}) copy-start(bf16[256,256]{1,0:T(8,128)(2,1)} %constant.8.clone.frames_ref) | copy-start | bytes 393220
  131.8 1.0 copy-start.6

commit v2 on v1

--- a/solution.py
+++ b/solution.py
@@ -58,12 +58,10 @@
 
 
 def lane_order():
-    m = np.zeros((512, 512), np.float32)
-    for fl in range(4):
-        for tl in range(4):
-            for i in range(32):
-                m[fl * 128 + tl * 32 + i, tl * 128 + fl * 32 + i] = 1
-    return m
+    row = lax.broadcasted_iota(jnp.int32, (512, 512), 0)
+    column = lax.broadcasted_iota(jnp.int32, (512, 512), 1)
+    goal = ((row >> 5) & 3) * 128 + (row >> 7) * 32 + (row & 31)
+    return (goal == column).astype(F32).astype(BF)
 
 
 def frames_of(phase):
@@ -178,10 +176,10 @@
     return pl.pallas_call(
         functools.partial(cut_kernel, [a for a, _ in ranges]),
         in_specs=[HB],
-        out_specs=[ANY] * len(ranges),
-        out_shape=[jax.ShapeDtypeStruct((IN_DEV, (b - a) * L), BF) for a, b in ranges],
+        out_specs=[VM] * len(ranges),
+        out_shape=[pltpu.VMEM((IN_DEV, (b - a) * L), BF) for a, b in ranges],
         scratch_shapes=[pltpu.SemaphoreType.DMA((len(ranges),))],
-        compiler_params=pltpu.CompilerParams(vmem_limit_bytes=MIB),
+        compiler_params=pltpu.CompilerParams(vmem_limit_bytes=4 * MIB),
         cost_estimate=pl.CostEstimate(flops=0, transcendentals=0, bytes_accessed=2 * MIB),
         name=name,
     )(pltpu.with_memory_space_constraint(voltages, pltpu.HBM))
@@ -275,16 +273,17 @@
 
 
 def pair_kernel(
-    flag_ref, lanes_ref, frames_ref, got_ref, weights, vis, beam, y, vis_buf, beam_buf, weight_ref, sem, beam_sem, weight_sem
+    flag_ref, frames_ref, got_ref, weights, vis, beam, y, vis_buf, beam_buf, weight_ref, sem, beam_sem, weight_sem
 ):
     dot = functools.partial(jnp.dot, preferred_element_type=F32)
     dot_t = lambda a, b: lax.dot_general(a, b, (((1,), (1,)), ((), ())), preferred_element_type=F32)
     fetches = [pltpu.make_async_copy(weights.at[s], weight_ref.at[s], weight_sem.at[s]) for s in range(SLOTS)]
     for fetch in fetches:
         fetch.start()
+    lanes = lane_order()
     for fh in range(4):
         parts = [got_ref[(fh * 4 + fl) * 8 : (fh * 4 + fl) * 8 + 8].reshape(512, 128) for fl in range(4)]
-        block = dot(jnp.concatenate(parts, 1), lanes_ref[...])
+        block = dot(jnp.concatenate(parts, 1), lanes)
         flag = flag_ref[:, fh * 128 : (fh + 1) * 128]
         for tl in range(4):
             y[fh * 4 + tl] = block[:, tl * 128 : (tl + 1) * 128] * flag
@@ -324,10 +323,10 @@
 
 
 def make_outputs(flags, got, weights):
-    consts = [jnp.asarray(m, BF) for m in (lane_order(), frame_order())]
+    frames = jnp.asarray(frame_order(), BF)
     return pl.pallas_call(
         pair_kernel,
-        in_specs=[VM] * 4 + [HB],
+        in_specs=[VM] * 3 + [HB],
         out_specs=[ANY, ANY],
         out_shape=[
             jax.ShapeDtypeStruct((SLOTS, 2, INPUTS, INPUTS), BF),
@@ -345,17 +344,16 @@
         compiler_params=pltpu.CompilerParams(vmem_limit_bytes=24 * MIB),
         cost_estimate=pl.CostEstimate(flops=5_000_000_000, transcendentals=0, bytes_accessed=16 * MIB),
         name="pairs",
-    )(flags, *consts, got, pltpu.with_memory_space_constraint(weights, pltpu.HBM))
+    )(flags, frames, got, pltpu.with_memory_space_constraint(weights, pltpu.HBM))
 
 
 def shards(voltages, station_flags, owner_map, beam_table, table_gains, table_delays):
     n_time = lax.axis_size("tm")
     up = lambda x: lax.ppermute(x, "tm", [(i, (i + 1) % n_time) for i in range(n_time)])
     down = lambda x: lax.ppermute(x, "tm", [(i, (i - 1) % n_time) for i in range(n_time)])
-    to_down, to_up = cut(voltages, [(0, 4), (13, 16)], "cut0")
-    n1, p1 = down(to_down), up(to_up)
-    to_down, to_up = cut(voltages, [(4, 8), (9, 13)], "cut1")
-    n2, p2 = down(to_down), up(to_up)
+    down0, up0, down1, up1 = cut(voltages, [(0, 4), (13, 16), (4, 8), (9, 13)], "cut")
+    n1, p1 = down(down0), up(up0)
+    n2, p2 = down(down1), up(up1)
     cos, sin = make_table(owner_map)
     taps = jnp.asarray(taps_table())
     first, held = make_spectra(0, (voltages, p1, n1, taps, cos, sin))

time: 144 us -> 88.7 us (0.62)
  Pallas kernels: 97.2 us -> 37.4 us
  waiting for transfers between devices: 22.1 us -> 28.3 us
    pallas_call x2 -> x1, Pallas kernels: 61.8 us -> 2.93 us  [cut(): pl.pallas_call(functools.partial(cut_kernel, [a for a, _ in ranges]), in_...]
    ppermute x2, waiting for transfers between devices: 0.01 us -> 6.26 us  [shards(): lax.ppermute(x, 'tm', [(i, (i + 1) % n_time) for i in range(n_time)])]
  transfers between devices with their start and end apart: 5 -> 5, of which waited for: 1 -> 3; matrix products, arithmetic and copies ran while one was open for 0% -> 1% of each run, Pallas kernels for 37% -> 23%
where the time goes in v2:
time: 88.7 us; the launch traced here: 88.4 us
  Pallas kernels  37.4 us (42%)
  waiting for transfers between devices  28.3 us (32%)
  starting transfers between devices  20.4 us (23%)
  between operations  0.98 us (1%)
    all_to_all x1, waiting for transfers between devices, shards(): lax.all_to_all(spectra, ('freq', 'tm'), split_axis=0, concat_axis=0, tile...  22.1 us
    pallas_call x2, Pallas kernels, make_spectra(): pl.pallas_call(functools.partial(spectra_kernel, phase), in_specs=[VM] *...  12.6 us
    ppermute x2, starting transfers between devices, shards(): lax.ppermute(x, 'tm', [(i, (i - 1) % n_time) for i in range(n_time)])  11.1 us
    pallas_call x1, Pallas kernels, make_outputs(): pl.pallas_call(pair_kernel, in_specs=[VM] * 3 + [HB], out_specs=[ANY, ANY...  10.5 us
    all_to_all x1, starting transfers between devices, shards(): lax.all_to_all(spectra, ('freq', 'tm'), split_axis=0, concat_axis=0, tile...  9.3 us
    pallas_call x1, Pallas kernels, make_weights(): pl.pallas_call(weight_kernel, in_specs=[SM, SM, VM, VM], out_specs=HB, ou...  7.89 us
    ppermute x2, waiting for transfers between devices, shards(): lax.ppermute(x, 'tm', [(i, (i + 1) % n_time) for i in range(n_time)])  6.26 us
    pallas_call x1, Pallas kernels, make_table(): pl.pallas_call(table_kernel, in_specs=[VM], out_specs=[VM, VM], out_shape...  3.58 us
  transfers between devices with their start and end apart: 5, of which 3 were waited for; matrix products, arithmetic and copies ran while one was open for 1% of the time, Pallas kernels for 23%

profile of v2, /device:TPU:1, one launch (start us, length us, event | category | flops | bytes accessed | tf_op | source)
XLA Modules:
  0.0 88.4 jit_solution(17590359908924428126)
XLA Ops:
  0.6 0.0 copy-start.1
  0.7 2.9 %cut.1 = (bf16[32,8192]{1,0:T(8,128)(2,1)}, bf16[32,6144]{1,0:T(8,128)(2,1)}, bf16[32,8192]{1,0:T(8,128)(2,1)}, bf16[32,8192]{1,0:T(8,128)(2,1)}) custom-call(bf16[32,32768]{1,0:T(8,128)(2,1)} %refs_0_.1), custom_call_target="tpu_custom_call" | custom-call | bytes 2097152 | tf_op jit(solution)/shard_map/cut/pallas_call | solution.py:176
  3.6 6.0 %collective-permute-start.3 = (bf16[32,8192]{1,0:T(8,128)(2,1)}, bf16[32,8192]{1,0:T(8,128)(2,1)}, u32[]{:S(2)}, u32[]{:S(2)}) collective-permute-start(bf16[32,8192]{1,0:T(8,128)(2,1)} %get-tuple-element.15), channel_id=1, source_target_pairs={{0,112},{16,0},{32,16},{48,32},{64,48},{80,64},{96,80},{112,96},{1... | collective-permute-start | bytes 1572872 | tf_op jit(solution)/shard_map/ppermute | solution.py:353
  9.6 5.1 %collective-permute-start.1 = (bf16[32,8192]{1,0:T(8,128)(2,1)}, bf16[32,8192]{1,0:T(8,128)(2,1)S(1)}, u32[]{:S(2)}, u32[]{:S(2)}) collective-permute-start(bf16[32,8192]{1,0:T(8,128)(2,1)} %get-tuple-element.11), channel_id=1, source_target_pairs={{0,112},{16,0},{32,16},{48,32},{64,48},{80,64},{96,80},{112,96},{1... | collective-permute-start | bytes 1572872 | tf_op jit(solution)/shard_map/ppermute | solution.py:353
  14.7 0.7 convert_element_type.19
  15.4 0.1 broadcast_in_dim.12
  15.5 0.2 broadcast_in_dim.13.chan_ref
  15.7 3.6 %table.1 = (bf16[1024,2048]{1,0:T(8,128)(2,1)S(1)}, bf16[1024,2048]{1,0:T(8,128)(2,1)S(1)}) custom-call(f32[8,16,8,128]{3,2,1,0:T(8,128)S(1)} %broadcast_in_dim.13.chan_ref), custom_call_target="tpu_custom_call" | custom-call | flops 33554432 | bytes 8388608 | tf_op jit(solution)/shard_map/table/pallas_call | solution.py:103
  19.3 3.9 %collective-permute-done.2.refs_1_ = bf16[32,6144]{1,0:T(8,128)(2,1)} collective-permute-done((bf16[32,6144]{1,0:T(8,128)(2,1)}, bf16[32,6144]{1,0:T(8,128)(2,1)}, u32[]{:S(2)}, u32[]{:S(2)}) %collective-permute-start.2) | collective-permute-done | bytes 393248 | tf_op jit(solution)/shard_map/ppermute | solution.py:352
  23.2 8.8 %spectra0.1 = (bf16[128,64,128]{2,1,0:T(8,128)(2,1)}, f32[256,2048]{1,0:T(8,128)S(1)}) custom-call(bf16[32,32768]{1,0:T(8,128)(2,1)S(1)} %copy-done, bf16[32,6144]{1,0:T(8,128)(2,1)} %collective-permute-done.2.refs_1_, bf16[32,8192]{1,0:T(8,128)(2,1)} %collective-permute-done.3.refs_2_, f32[16,2048]{1,0:T(8,128)S(1)} %copy-done.1, ...), custom_call_target="tpu_custom_call" | custom-call | flops 2147483648 | bytes 12582912 | tf_op jit(solution)/shard_map/spectra0/pallas_call | solution.py:258
  32.0 2.3 %collective-permute-done.refs_0_ = bf16[32,8192]{1,0:T(8,128)(2,1)S(1)} collective-permute-done((bf16[32,8192]{1,0:T(8,128)(2,1)}, bf16[32,8192]{1,0:T(8,128)(2,1)S(1)}, u32[]{:S(2)}, u32[]{:S(2)}) %collective-permute-start) | collective-permute-done | bytes 524320 | tf_op jit(solution)/shard_map/ppermute | solution.py:352
  34.3 3.8 %spectra1.1 = bf16[128,64,128]{2,1,0:T(8,128)(2,1)} custom-call(bf16[32,8192]{1,0:T(8,128)(2,1)S(1)} %collective-permute-done.refs_0_, bf16[32,8192]{1,0:T(8,128)(2,1)S(1)} %collective-permute-done.1.refs_1_, f32[16,2048]{1,0:T(8,128)S(1)} %copy-done.1, bf16[1024,2048]{1,0:T(8,128)(2,1)S(1)} %get-tuple-element.12.refs_4_.refs_3_, ...), custom_call_target="tpu_custom_call", output_to_operand_aliasing={{}: (6, {})} | custom-call | flops 2147483648 | bytes 12582912 | tf_op jit(solution)/shard_map/spectra1/pallas_call | solution.py:258
  38.1 0.0 copy-start.7
  38.1 0.0 copy-start.2
  38.2 0.0 copy-start.3
  38.2 0.0 copy-start.4
  38.2 0.0 copy-start.5
  38.2 9.3 %all-to-all-start = ((bf16[128,64,128]{2,1,0:T(8,128)(2,1)}), bf16[128,64,128]{2,1,0:T(8,128)(2,1)S(1)}, u32[]{:S(2)}, u32[]{:S(2)}) async-start(bf16[128,64,128]{2,1,0:T(8,128)(2,1)} %spectra1.1), calls=%async_computation | async-start | bytes 4194304 | tf_op jit(solution)/shard_map/all_to_all | solution.py:363
  47.5 0.1 broadcast_in_dim.11
  47.6 0.1 convert_element_type.18.flag_ref
  47.8 0.0 copy-start.6
  47.8 7.9 %weights.1 = bf16[8,2,256,512]{3,2,1,0:T(8,128)(2,1)} custom-call(s32[1024]{0:T(1024)S(1)} %copy-done.4, s32[256]{0:T(256)S(1)} %copy-done.5, f32[256,512]{1,0:T(8,128)S(1)} %copy-done.2, f32[256,512]{1,0:T(8,128)S(1)} %copy-done.3), custom_call_target="tpu_custom_call" | custom-call | flops 52428800 | bytes 6291456 | tf_op jit(solution)/shard_map/weights/pallas_call | solution.py:146
  55.7 22.1 %all-to-all-done.got_ref = bf16[128,64,128]{2,1,0:T(8,128)(2,1)S(1)} async-done(((bf16[128,64,128]{2,1,0:T(8,128)(2,1)}), bf16[128,64,128]{2,1,0:T(8,128)(2,1)S(1)}, u32[]{:S(2)}, u32[]{:S(2)}) %all-to-all-start) | async-done | bytes 2097184 | tf_op jit(solution)/shard_map/all_to_all | solution.py:363
  77.8 10.5 %pairs.1 = (bf16[8,2,512,512]{3,2,1,0:T(8,128)(2,1)}, bf16[8,128,2,256]{3,2,1,0:T(2,128)(2,1)}) custom-call(f32[1,512]{1,0:T(1,128)S(1)} %convert_element_type.18.flag_ref, bf16[256,256]{1,0:T(8,128)(2,1)S(1)} %copy-done.6, bf16[128,64,128]{2,1,0:T(8,128)(2,1)S(1)} %all-to-all-done.got_ref, bf16[8,2,256,512]{3,2,1,0:T(8,128)(2,1)} %weights.1), custom_call_target="tpu_custom_call" | custom-call | flops 5000000000 | bytes 16777216 | tf_op jit(solution)/shard_map/pairs/pallas_call | solution.py:327
  (14 shorter events, 0.0 us)
Async XLA Ops:
  0.6 22.6 %copy-start.1 = (f32[16,2048]{1,0:T(8,128)S(1)}, f32[16,2048]{1,0:T(8,128)}, u32[]{:S(2)}) copy-start(f32[16,2048]{1,0:T(8,128)} %constant.4.clone.refs_3_.refs_2_) | copy-start | bytes 393220
  0.6 22.6 %copy-start = (bf16[32,32768]{1,0:T(8,128)(2,1)S(1)}, bf16[32,32768]{1,0:T(8,128)(2,1)}, u32[]{:S(2)}) copy-start(bf16[32,32768]{1,0:T(8,128)(2,1)} %refs_0_.1) | copy-start | bytes 6291460
  3.6 19.6 %collective-permute-start.3 = (bf16[32,8192]{1,0:T(8,128)(2,1)}, bf16[32,8192]{1,0:T(8,128)(2,1)}, u32[]{:S(2)}, u32[]{:S(2)}) collective-permute-start(bf16[32,8192]{1,0:T(8,128)(2,1)} %get-tuple-element.15), channel_id=1, source_target_pairs={{0,112},{16,0},{32,16},{48,32},{64,48},{80,64},{96,80},{112,96},{1... | collective-permute-start | bytes 1572872 | tf_op jit(solution)/shard_map/ppermute | solution.py:353
  9.6 13.6 %collective-permute-start.2 = (bf16[32,6144]{1,0:T(8,128)(2,1)}, bf16[32,6144]{1,0:T(8,128)(2,1)}, u32[]{:S(2)}, u32[]{:S(2)}) collective-permute-start(bf16[32,6144]{1,0:T(8,128)(2,1)} %get-tuple-element.14), channel_id=1, source_target_pairs={{0,16},{16,32},{32,48},{48,64},{64,80},{80,96},{96,112},{112,0},{1... | collective-permute-start | bytes 1179656 | tf_op jit(solution)/shard_map/ppermute | solution.py:352
  9.6 24.7 %collective-permute-start = (bf16[32,8192]{1,0:T(8,128)(2,1)}, bf16[32,8192]{1,0:T(8,128)(2,1)S(1)}, u32[]{:S(2)}, u32[]{:S(2)}) collective-permute-start(bf16[32,8192]{1,0:T(8,128)(2,1)} %get-tuple-element.10), channel_id=1, source_target_pairs={{0,16},{16,32},{32,48},{48,64},{64,80},{80,96},{96,112},{112,0},{1... | collective-permute-start | bytes 1572872 | tf_op jit(solution)/shard_map/ppermute | solution.py:352
  9.6 24.7 %collective-permute-start.1 = (bf16[32,8192]{1,0:T(8,128)(2,1)}, bf16[32,8192]{1,0:T(8,128)(2,1)S(1)}, u32[]{:S(2)}, u32[]{:S(2)}) collective-permute-start(bf16[32,8192]{1,0:T(8,128)(2,1)} %get-tuple-element.11), channel_id=1, source_target_pairs={{0,112},{16,0},{32,16},{48,32},{64,48},{80,64},{96,80},{112,96},{1... | collective-permute-start | bytes 1572872 | tf_op jit(solution)/shard_map/ppermute | solution.py:353
  38.1 9.4 %copy-start.7 = (s32[256]{0:T(256)S(1)}, s32[256]{0:T(256)}, u32[]{:S(2)}) copy-start(s32[256]{0:T(256)} %param.9) | copy-start | bytes 3076
  38.1 9.6 %copy-start.2 = (f32[256,512]{1,0:T(8,128)S(1)}, f32[256,512]{1,0:T(8,128)}, u32[]{:S(2)}) copy-start(f32[256,512]{1,0:T(8,128)} %gains_ref.1) | copy-start | bytes 1572868
  38.2 9.6 %copy-start.3 = (f32[256,512]{1,0:T(8,128)S(1)}, f32[256,512]{1,0:T(8,128)}, u32[]{:S(2)}) copy-start(f32[256,512]{1,0:T(8,128)} %delays_ref.1) | copy-start | bytes 1572868
  38.2 9.6 %copy-start.4 = (s32[1024]{0:T(1024)S(1)}, s32[1024]{0:T(1024)}, u32[]{:S(2)}) copy-start(s32[1024]{0:T(1024)} %owner_ref.1) | copy-start | bytes 12292
  38.2 9.6 %copy-start.5 = (s32[256]{0:T(256)S(1)}, s32[256]{0:T(256)}, u32[]{:S(2)}) copy-start(s32[256]{0:T(256)} %beam_ref.1) | copy-start | bytes 3076
  38.2 39.6 %all-to-all-start = ((bf16[128,64,128]{2,1,0:T(8,128)(2,1)}), bf16[128,64,128]{2,1,0:T(8,128)(2,1)S(1)}, u32[]{:S(2)}, u32[]{:S(2)}) async-start(bf16[128,64,128]{2,1,0:T(8,128)(2,1)} %spectra1.1), calls=%async_computation | async-start | bytes 4194304 | tf_op jit(solution)/shard_map/all_to_all | solution.py:363
  47.8 30.0 %copy-start.6 = (bf16[256,256]{1,0:T(8,128)(2,1)S(1)}, bf16[256,256]{1,0:T(8,128)(2,1)}, u32[]{:S(2)}) copy-start(bf16[256,256]{1,0:T(8,128)(2,1)} %constant.5.clone.frames_ref) | copy-start | bytes 393220

commit v3 on v2

--- a/solution.py
+++ b/solution.py
@@ -34,7 +34,7 @@
 
 
 COS = fit(lambda r: np.cos(2 * np.pi * r), 6)
-NEG_SIN = fit(lambda r: -np.sin(2 * np.pi * r) / r, 6)
+NEG_SIN = fit(lambda r: -np.sin(2 * np.pi * r) / r, 5)
 
 
 def horner(coefs, z):
@@ -81,9 +81,15 @@
     return m
 
 
-def table_kernel(chan_ref, cos_ref, sin_ref):
+def table_kernel(owner_ref, cos_ref, sin_ref, chans):
+    turned = owner_ref[...].astype(F32).T
+    for f in range(16):
+        for t in range(8):
+            column = turned[f * SLOTS : (f + 1) * SLOTS, t : t + 1]
+            chans[f * 64 + t * SLOTS : f * 64 + (t + 1) * SLOTS, :] = jnp.broadcast_to(column, (SLOTS, 128))
+
     def group(g, carry):
-        chan = chan_ref[:, g].reshape(64, 128)
+        chan = chans[pl.ds(pl.multiple_of(g * 64, 64), 64), :]
         n2 = lax.broadcasted_iota(jnp.int32, (64, 128), 1).astype(F32)
         c, s = cos_negsin(chan * n2 * (1.0 / L))
         a, b = cos_negsin(chan * (128.0 / L))
@@ -99,19 +105,19 @@
 
 
 def make_table(owner_map):
-    chan = jnp.broadcast_to(owner_map.astype(F32)[:, None], (CH, 128)).reshape(8, 16, SLOTS, 128)
     return pl.pallas_call(
         table_kernel,
         in_specs=[VM],
         out_specs=[VM, VM],
         out_shape=[pltpu.VMEM((CH, L), BF)] * 2,
+        scratch_shapes=[pltpu.VMEM((CH, 128), F32)],
         cost_estimate=pl.CostEstimate(flops=16 * CH * L, transcendentals=0, bytes_accessed=8 * MIB),
         compiler_params=pltpu.CompilerParams(vmem_limit_bytes=4 * MIB),
         name="table",
-    )(chan)
-
-
-def weight_kernel(owner_ref, beam_ref, gains_ref, delays_ref, out_ref, gain, delay, made, sem):
+    )(owner_map.reshape(8, 128))
+
+
+def weight_kernel(owner_ref, beam_ref, gains_ref, delays_ref, out_ref, gain, delay):
     def pick(g, carry):
         for j in range(8):
             b = g * 8 + j
@@ -123,39 +129,28 @@
     lax.fori_loop(0, BEAMS // 8, pick, 0)
     start = (lax.axis_index("tm") * 16 + lax.axis_index("freq")) * SLOTS
 
-    copies = []
-    for s in range(SLOTS):
+    def group(g, carry):
+        s = g // (BEAMS // 64)
+        at = pl.ds(pl.multiple_of(g % (BEAMS // 64) * 64, 64), 64)
         chan = owner_ref[start + s].astype(F32) * (1.0 / L)
-
-        def group(g, carry):
-            at = pl.ds(pl.multiple_of(g * 32, 32), 32)
-            c, n = cos_negsin(delay[at, :] * chan)
-            scaled = gain[at, :] * (1.0 / math.sqrt(INPUTS))
-            made[s, 0, at, :] = (scaled * c).astype(BF)
-            made[s, 1, at, :] = (scaled * n).astype(BF)
-            return carry
-
-        lax.fori_loop(0, BEAMS // 32, group, 0)
-        copies.append(pltpu.make_async_copy(made.at[s], out_ref.at[s], sem.at[s]))
-        copies[-1].start()
-    for copy in copies:
-        copy.wait()
+        c, n = cos_negsin(delay[at, :] * chan)
+        scaled = gain[at, :] * (1.0 / math.sqrt(INPUTS))
+        out_ref[s, 0, at, :] = (scaled * c).astype(BF)
+        out_ref[s, 1, at, :] = (scaled * n).astype(BF)
+        return carry
+
+    lax.fori_loop(0, SLOTS * BEAMS // 64, group, 0)
 
 
 def make_weights(owner_map, beam_table, gains, delays):
     return pl.pallas_call(
         weight_kernel,
         in_specs=[SM, SM, VM, VM],
-        out_specs=HB,
-        out_shape=pltpu.HBM((SLOTS, 2, BEAMS, INPUTS), BF),
-        scratch_shapes=[
-            pltpu.VMEM((BEAMS, INPUTS), F32),
-            pltpu.VMEM((BEAMS, INPUTS), F32),
-            pltpu.VMEM((SLOTS, 2, BEAMS, INPUTS), BF),
-            pltpu.SemaphoreType.DMA((SLOTS,)),
-        ],
+        out_specs=VM,
+        out_shape=pltpu.VMEM((SLOTS, 2, BEAMS, INPUTS), BF),
+        scratch_shapes=[pltpu.VMEM((BEAMS, INPUTS), F32)] * 2,
         cost_estimate=pl.CostEstimate(flops=50 * SLOTS * INPUTS * BEAMS, transcendentals=0, bytes_accessed=6 * MIB),
-        compiler_params=pltpu.CompilerParams(vmem_limit_bytes=8 * MIB),
+        compiler_params=pltpu.CompilerParams(vmem_limit_bytes=4 * MIB),
         name="weights",
     )(owner_map, beam_table, gains, delays)
 
@@ -187,10 +182,10 @@
 
 def spectra_kernel(phase, *refs):
     if phase == 0:
-        own, p1, n1, taps_ref, cos_ref, sin_ref, out, held, filt, message, sem = refs
+        own, p1, n1, taps_ref, cos_ref, sin_ref, *_, out, held, filt, message, sem = refs
         p2 = n2 = None
     else:
-        p2, n2, taps_ref, cos_ref, sin_ref, held, _, out, filt, message, sem = refs
+        p2, n2, taps_ref, cos_ref, sin_ref, held, *_, out, filt, message, sem = refs
         own = p1 = n1 = None
     pieces = [(p2, f) for f in range(4)] + [(p1, f) for f in range(3)] + [(own, f) for f in range(FR)]
     pieces += [(n1, f) for f in range(4)] + [(n2, f) for f in range(4)]
@@ -252,13 +247,14 @@
         copy.wait()
 
 
-def make_spectra(phase, args, before=None):
-    args = [*args] + ([] if before is None else [before])
-    out = pltpu.HBM((128, 64, 128), BF)
+def make_spectra(phase, args, after=()):
+    ready = len(args)
+    args = [*args, *after]
+    out = pltpu.VMEM((128, 64, 128), BF)
     return pl.pallas_call(
         functools.partial(spectra_kernel, phase),
-        in_specs=[VM] * (len(args) - 1) + [HB if phase else VM],
-        out_specs=HB if phase else [HB, VM],
+        in_specs=[VM] * ready + [ANY] * len(after),
+        out_specs=ANY if phase else [ANY, VM],
         out_shape=out if phase else [out, pltpu.VMEM((8 * IN_DEV, L), F32)],
         input_output_aliases={len(args) - 1: 0} if phase else {},
         scratch_shapes=[
@@ -273,18 +269,19 @@
 
 
 def pair_kernel(
-    flag_ref, frames_ref, got_ref, weights, vis, beam, y, vis_buf, beam_buf, weight_ref, sem, beam_sem, weight_sem
+    flag_ref, frames_ref, got_ref, weight_ref, vis, beam, y, vis_buf, beam_buf, sem, beam_sem
 ):
     dot = functools.partial(jnp.dot, preferred_element_type=F32)
     dot_t = lambda a, b: lax.dot_general(a, b, (((1,), (1,)), ((), ())), preferred_element_type=F32)
-    fetches = [pltpu.make_async_copy(weights.at[s], weight_ref.at[s], weight_sem.at[s]) for s in range(SLOTS)]
-    for fetch in fetches:
-        fetch.start()
     lanes = lane_order()
+    station = lax.broadcasted_iota(jnp.int32, (INPUTS // 2, INPUTS), 0)
+    twice = (station == lax.broadcasted_iota(jnp.int32, (INPUTS // 2, INPUTS), 1) >> 1).astype(F32).astype(BF)
+    used = jnp.broadcast_to(flag_ref[...].astype(F32), (8, INPUTS // 2)).astype(BF)
+    flags = dot(used, twice)[0:1]
     for fh in range(4):
         parts = [got_ref[(fh * 4 + fl) * 8 : (fh * 4 + fl) * 8 + 8].reshape(512, 128) for fl in range(4)]
         block = dot(jnp.concatenate(parts, 1), lanes)
-        flag = flag_ref[:, fh * 128 : (fh + 1) * 128]
+        flag = flags[:, fh * 128 : (fh + 1) * 128]
         for tl in range(4):
             y[fh * 4 + tl] = block[:, tl * 128 : (tl + 1) * 128] * flag
     copies = {}
@@ -308,10 +305,10 @@
             vis_buf[b, c] = (dot(left, w) * (1.0 / 128)).astype(BF)
             started.append(pltpu.make_async_copy(vis_buf.at[b, c], vis.at[s, c], sem.at[b, c]))
             started[-1].start()
-        fetches[s].wait()
         w_re, w_im = weight_ref[s, 0], weight_ref[s, 1]
-        b_re = dot_t(z[0], w_re) + dot_t(-z[1], w_im)
-        b_im = dot_t(z[0], w_im) + dot_t(z[1], w_re)
+        by_re, by_im = dot_t(w, w_re), dot_t(w, w_im)
+        b_re = by_re[:128] - by_im[128:]
+        b_im = by_im[:128] + by_re[128:]
         both = jnp.concatenate([b_re, b_im], 0).astype(BF)
         beam_buf[b] = dot(frames_ref[...], both).astype(BF).reshape(128, 2, BEAMS)
         started.append(pltpu.make_async_copy(beam_buf.at[b], beam.at[s], beam_sem.at[b]))
@@ -326,7 +323,7 @@
     frames = jnp.asarray(frame_order(), BF)
     return pl.pallas_call(
         pair_kernel,
-        in_specs=[VM] * 3 + [HB],
+        in_specs=[VM] * 4,
         out_specs=[ANY, ANY],
         out_shape=[
             jax.ShapeDtypeStruct((SLOTS, 2, INPUTS, INPUTS), BF),
@@ -336,15 +333,13 @@
             pltpu.VMEM((16, 512, 128), F32),
             pltpu.VMEM((SLOTS, 2, INPUTS, INPUTS), BF),
             pltpu.VMEM((SLOTS, 128, 2, BEAMS), BF),
-            pltpu.VMEM((SLOTS, 2, BEAMS, INPUTS), BF),
             pltpu.SemaphoreType.DMA((SLOTS, 2)),
             pltpu.SemaphoreType.DMA((SLOTS,)),
-            pltpu.SemaphoreType.DMA((SLOTS,)),
         ],
-        compiler_params=pltpu.CompilerParams(vmem_limit_bytes=24 * MIB),
+        compiler_params=pltpu.CompilerParams(vmem_limit_bytes=20 * MIB),
         cost_estimate=pl.CostEstimate(flops=5_000_000_000, transcendentals=0, bytes_accessed=16 * MIB),
         name="pairs",
-    )(flags, frames, got, pltpu.with_memory_space_constraint(weights, pltpu.HBM))
+    )(flags, frames, got, weights)
 
 
 def shards(voltages, station_flags, owner_map, beam_table, table_gains, table_delays):
@@ -356,10 +351,10 @@
     n2, p2 = down(down1), up(up1)
     cos, sin = make_table(owner_map)
     taps = jnp.asarray(taps_table())
-    first, held = make_spectra(0, (voltages, p1, n1, taps, cos, sin))
-    spectra = make_spectra(1, (p2, n2, taps, cos, sin, held), first)
     weights = make_weights(owner_map, beam_table, table_gains, table_delays)
-    flags = jnp.repeat(station_flags, 2).astype(F32).reshape(1, INPUTS)
+    flags = station_flags.reshape(1, INPUTS // 2)
+    first, held = make_spectra(0, (voltages, p1, n1, taps, cos, sin), (weights,))
+    spectra = make_spectra(1, (p2, n2, taps, cos, sin, held), (first,))
     got = lax.all_to_all(spectra, ("freq", "tm"), split_axis=0, concat_axis=0, tiled=True)
     return make_outputs(flags, got, weights)
 

time: 88.7 us -> 85.3 us (0.962)
  blocking collectives: 0 us -> 39.4 us
  waiting for transfers between devices: 28.3 us -> 0.93 us
  starting transfers between devices: 20.4 us -> 11.1 us
  Pallas kernels: 37.4 us -> 32.7 us
    all_to_all x0 -> x1, blocking collectives: none -> 39.4 us  [shards(): lax.all_to_all(spectra, ('freq', 'tm'), split_axis=0, concat_axis=0, tile...]
    all_to_all x1 -> x0, waiting for transfers between devices: 22.1 us -> none  [shards(): lax.all_to_all(spectra, ('freq', 'tm'), split_axis=0, concat_axis=0, tile...]
    all_to_all x1 -> x0, starting transfers between devices: 9.3 us -> none  [shards(): lax.all_to_all(spectra, ('freq', 'tm'), split_axis=0, concat_axis=0, tile...]
    ppermute x2, waiting for transfers between devices: 6.26 us -> 0.92 us  [shards(): lax.ppermute(x, 'tm', [(i, (i + 1) % n_time) for i in range(n_time)])]
    pallas_call x2, Pallas kernels: 18.3 us -> 15.8 us  [the longest x1 8.94 us: make_outputs(): pl.pallas_call(pair_kernel, in_specs=[VM] * 4, out_specs=[ANY, ANY], out_...]
    pallas_call x1, Pallas kernels: 2.93 us -> 1.6 us  [cut(): pl.pallas_call(functools.partial(cut_kernel, [a for a, _ in ranges]), in_...]
    pallas_call x2, Pallas kernels: 12.6 us -> 11.5 us  [make_spectra(): pl.pallas_call(functools.partial(spectra_kernel, phase), in_specs=[VM] *...]
  transfers between devices with their start and end apart: 5 -> 4, of which waited for: 3 -> 1; matrix products, arithmetic and copies ran while one was open for 1% -> 0% of each run, Pallas kernels for 23% -> 22%
where the time goes in v3:
time: 85.3 us; the launch traced here: 85.2 us
  blocking collectives  39.4 us (46%)
  Pallas kernels  32.7 us (38%)
  starting transfers between devices  11.1 us (13%)
  between operations  0.95 us (1%)
  waiting for transfers between devices  0.93 us (1%)
    all_to_all x1, blocking collectives, shards(): lax.all_to_all(spectra, ('freq', 'tm'), split_axis=0, concat_axis=0, tile...  39.4 us
    pallas_call x2, Pallas kernels, make_spectra(): pl.pallas_call(functools.partial(spectra_kernel, phase), in_specs=[VM] *...  11.5 us
    ppermute x2, starting transfers between devices, shards(): lax.ppermute(x, 'tm', [(i, (i - 1) % n_time) for i in range(n_time)])  11.1 us
    pallas_call x1, Pallas kernels, make_outputs(): pl.pallas_call(pair_kernel, in_specs=[VM] * 4, out_specs=[ANY, ANY], out_...  8.94 us
    pallas_call x1, Pallas kernels, make_weights(): pl.pallas_call(weight_kernel, in_specs=[SM, SM, VM, VM], out_specs=VM, ou...  6.82 us
    pallas_call x1, Pallas kernels, make_table(): pl.pallas_call(table_kernel, in_specs=[VM], out_specs=[VM, VM], out_shape...  3.89 us
  transfers between devices with their start and end apart: 4, of which 1 were waited for; matrix products, arithmetic and copies ran while one was open for 0% of the time, Pallas kernels for 22%

profile of v3, /device:TPU:1, one launch (start us, length us, event | category | flops | bytes accessed | tf_op | source)
XLA Modules:
  0.0 85.2 jit_solution(4209325629356182132)
XLA Ops:
  0.7 1.6 %cut.1 = (bf16[32,8192]{1,0:T(8,128)(2,1)S(1)}, bf16[32,6144]{1,0:T(8,128)(2,1)S(1)}, bf16[32,8192]{1,0:T(8,128)(2,1)S(1)}, bf16[32,8192]{1,0:T(8,128)(2,1)S(1)}) custom-call(bf16[32,32768]{1,0:T(8,128)(2,1)} %refs_0_.1), custom_call_target="tpu_custom_call" | custom-call | bytes 2097152 | tf_op jit(solution)/shard_map/cut/pallas_call | solution.py:171
  2.3 6.0 %collective-permute-start.3 = (bf16[32,8192]{1,0:T(8,128)(2,1)S(1)}, bf16[32,8192]{1,0:T(8,128)(2,1)S(1)}, u32[]{:S(2)}, u32[]{:S(2)}) collective-permute-start(bf16[32,8192]{1,0:T(8,128)(2,1)S(1)} %get-tuple-element.15), channel_id=1, source_target_pairs={{0,112},{16,0},{32,16},{48,32},{64,48},{80,64},{96,80},{112,96},{1... | collective-permute-start | bytes 1572872 | tf_op jit(solution)/shard_map/ppermute | solution.py:348
  8.3 0.0 collective-permute-start.2
  8.3 0.0 collective-permute-start
  8.3 5.1 %collective-permute-start.1 = (bf16[32,8192]{1,0:T(8,128)(2,1)S(1)}, bf16[32,8192]{1,0:T(8,128)(2,1)S(1)}, u32[]{:S(2)}, u32[]{:S(2)}) collective-permute-start(bf16[32,8192]{1,0:T(8,128)(2,1)S(1)} %get-tuple-element.11), channel_id=1, source_target_pairs={{0,112},{16,0},{32,16},{48,32},{64,48},{80,64},{96,80},{112,96},{1... | collective-permute-start | bytes 1572872 | tf_op jit(solution)/shard_map/ppermute | solution.py:348
  13.4 3.9 %table.1 = (bf16[1024,2048]{1,0:T(8,128)(2,1)S(1)}, bf16[1024,2048]{1,0:T(8,128)(2,1)S(1)}) custom-call(s32[8,128]{1,0:T(8,128)S(1)} %bitcast.2), custom_call_target="tpu_custom_call" | custom-call | flops 33554432 | bytes 8388608 | tf_op jit(solution)/shard_map/table/pallas_call | solution.py:108
  17.3 0.0 copy-done.3
  17.3 0.0 copy-done.2
  17.3 0.0 copy-done.5
  17.3 0.0 copy-start
  17.3 0.0 copy-start.1
  17.4 6.8 %weights.1.refs_6_.weight_ref = bf16[8,2,256,512]{3,2,1,0:T(8,128)(2,1)S(1)} custom-call(s32[1024]{0:T(1024)S(1)} %copy-done.4, s32[256]{0:T(256)S(1)} %copy-done.5, f32[256,512]{1,0:T(8,128)S(1)} %copy-done.2, f32[256,512]{1,0:T(8,128)S(1)} %copy-done.3), custom_call_target="tpu_custom_call" | custom-call | flops 52428800 | bytes 6291456 | tf_op jit(solution)/shard_map/weights/pallas_call | solution.py:146
  24.2 0.0 collective-permute-done.2.refs_1_
  24.2 0.0 collective-permute-done.3.refs_2_
  24.2 0.0 copy-done
  24.2 0.0 copy-done.1
  24.2 7.7 %spectra0.1 = (bf16[128,64,128]{2,1,0:T(8,128)(2,1)S(1)}, f32[256,2048]{1,0:T(8,128)S(1)}) custom-call(bf16[32,32768]{1,0:T(8,128)(2,1)S(1)} %copy-done, bf16[32,6144]{1,0:T(8,128)(2,1)S(1)} %collective-permute-done.2.refs_1_, bf16[32,8192]{1,0:T(8,128)(2,1)S(1)} %collective-permute-done.3.refs_2_, f32[16,2048]{1,0:T(8,128)S(1)} %copy-done.1, ...), custom_call_target="tpu_custom_call" | custom-call | flops 2147483648 | bytes 12582912 | tf_op jit(solution)/shard_map/spectra0/pallas_call | solution.py:254
  31.9 0.9 %collective-permute-done.refs_0_ = bf16[32,8192]{1,0:T(8,128)(2,1)S(1)} collective-permute-done((bf16[32,8192]{1,0:T(8,128)(2,1)S(1)}, bf16[32,8192]{1,0:T(8,128)(2,1)S(1)}, u32[]{:S(2)}, u32[]{:S(2)}) %collective-permute-start) | collective-permute-done | bytes 524320 | tf_op jit(solution)/shard_map/ppermute | solution.py:347
  32.8 0.0 collective-permute-done.1.refs_1_
  32.8 3.8 %spectra1.1 = bf16[128,64,128]{2,1,0:T(8,128)(2,1)S(1)} custom-call(bf16[32,8192]{1,0:T(8,128)(2,1)S(1)} %collective-permute-done.refs_0_, bf16[32,8192]{1,0:T(8,128)(2,1)S(1)} %collective-permute-done.1.refs_1_, f32[16,2048]{1,0:T(8,128)S(1)} %copy-done.1, bf16[1024,2048]{1,0:T(8,128)(2,1)S(1)} %get-tuple-element.12.refs_4_.refs_3_, ...), custom_call_target="tpu_custom_call", output_to_operand_aliasing={{}: (6, {})} | custom-call | flops 2147483648 | bytes 12582912 | tf_op jit(solution)/shard_map/spectra1/pallas_call | solution.py:254
  36.6 0.0 copy-start.6
  36.6 0.0 copy-start.7
  36.7 39.4 %all_to_all.5.got_ref = bf16[128,64,128]{2,1,0:T(8,128)(2,1)S(1)} all-to-all(bf16[128,64,128]{2,1,0:T(8,128)(2,1)S(1)} %spectra1.1), channel_id=1, replica_groups=mesh['tm'=8,'freq'=16] {'freq','tm'}, dimensions={0} | all-to-all | bytes 4194304 | tf_op jit(solution)/shard_map/all_to_all | solution.py:358
  76.1 8.9 %pairs.1 = (bf16[8,2,512,512]{3,2,1,0:T(8,128)(2,1)}, bf16[8,128,2,256]{3,2,1,0:T(2,128)(2,1)}) custom-call(s32[1,256]{1,0:T(1,128)S(1)} %bitcast.3, bf16[256,256]{1,0:T(8,128)(2,1)S(1)} %copy-done.7, bf16[128,64,128]{2,1,0:T(8,128)(2,1)S(1)} %all_to_all.5.got_ref, bf16[8,2,256,512]{3,2,1,0:T(8,128)(2,1)S(1)} %weights.1.refs_6_.weight_ref), custom_call_target="tpu_custom_call" | custom-call | flops 5000000000 | bytes 16777216 | tf_op jit(solution)/shard_map/pairs/pallas_call | solution.py:324
  (7 shorter events, 0.0 us)
Async XLA Ops:
  0.6 12.8 %copy-start.4 = (s32[1024]{0:T(1024)S(1)}, s32[1024]{0:T(1024)}, u32[]{:S(2)}) copy-start(s32[1024]{0:T(1024)} %owner_ref.1) | copy-start | bytes 12292
  0.6 16.7 %copy-start.3 = (f32[256,512]{1,0:T(8,128)S(1)}, f32[256,512]{1,0:T(8,128)}, u32[]{:S(2)}) copy-start(f32[256,512]{1,0:T(8,128)} %delays_ref.1) | copy-start | bytes 1572868
  0.7 16.7 %copy-start.2 = (f32[256,512]{1,0:T(8,128)S(1)}, f32[256,512]{1,0:T(8,128)}, u32[]{:S(2)}) copy-start(f32[256,512]{1,0:T(8,128)} %gains_ref.1) | copy-start | bytes 1572868
  0.7 16.7 %copy-start.5 = (s32[256]{0:T(256)S(1)}, s32[256]{0:T(256)}, u32[]{:S(2)}) copy-start(s32[256]{0:T(256)} %beam_ref.1) | copy-start | bytes 3076
  2.3 21.9 %collective-permute-start.3 = (bf16[32,8192]{1,0:T(8,128)(2,1)S(1)}, bf16[32,8192]{1,0:T(8,128)(2,1)S(1)}, u32[]{:S(2)}, u32[]{:S(2)}) collective-permute-start(bf16[32,8192]{1,0:T(8,128)(2,1)S(1)} %get-tuple-element.15), channel_id=1, source_target_pairs={{0,112},{16,0},{32,16},{48,32},{64,48},{80,64},{96,80},{112,96},{1... | collective-permute-start | bytes 1572872 | tf_op jit(solution)/shard_map/ppermute | solution.py:348
  8.3 15.9 %collective-permute-start.2 = (bf16[32,6144]{1,0:T(8,128)(2,1)S(1)}, bf16[32,6144]{1,0:T(8,128)(2,1)S(1)}, u32[]{:S(2)}, u32[]{:S(2)}) collective-permute-start(bf16[32,6144]{1,0:T(8,128)(2,1)S(1)} %get-tuple-element.14), channel_id=1, source_target_pairs={{0,16},{16,32},{32,48},{48,64},{64,80},{80,96},{96,112},{112,0},{1... | collective-permute-start | bytes 1179656 | tf_op jit(solution)/shard_map/ppermute | solution.py:347
  8.3 24.5 %collective-permute-start = (bf16[32,8192]{1,0:T(8,128)(2,1)S(1)}, bf16[32,8192]{1,0:T(8,128)(2,1)S(1)}, u32[]{:S(2)}, u32[]{:S(2)}) collective-permute-start(bf16[32,8192]{1,0:T(8,128)(2,1)S(1)} %get-tuple-element.10), channel_id=1, source_target_pairs={{0,16},{16,32},{32,48},{48,64},{64,80},{80,96},{96,112},{112,0},{1... | collective-permute-start | bytes 1572872 | tf_op jit(solution)/shard_map/ppermute | solution.py:347
  8.3 24.5 %collective-permute-start.1 = (bf16[32,8192]{1,0:T(8,128)(2,1)S(1)}, bf16[32,8192]{1,0:T(8,128)(2,1)S(1)}, u32[]{:S(2)}, u32[]{:S(2)}) collective-permute-start(bf16[32,8192]{1,0:T(8,128)(2,1)S(1)} %get-tuple-element.11), channel_id=1, source_target_pairs={{0,112},{16,0},{32,16},{48,32},{64,48},{80,64},{96,80},{112,96},{1... | collective-permute-start | bytes 1572872 | tf_op jit(solution)/shard_map/ppermute | solution.py:348
  17.3 6.9 %copy-start = (bf16[32,32768]{1,0:T(8,128)(2,1)S(1)}, bf16[32,32768]{1,0:T(8,128)(2,1)}, u32[]{:S(2)}) copy-start(bf16[32,32768]{1,0:T(8,128)(2,1)} %refs_0_.1) | copy-start | bytes 6291460
  17.3 6.9 %copy-start.1 = (f32[16,2048]{1,0:T(8,128)S(1)}, f32[16,2048]{1,0:T(8,128)}, u32[]{:S(2)}) copy-start(f32[16,2048]{1,0:T(8,128)} %constant.4.clone.refs_3_.refs_2_) | copy-start | bytes 393220
  36.6 39.4 %copy-start.6 = (s32[256]{0:T(256)S(1)}, s32[256]{0:T(256)}, u32[]{:S(2)}) copy-start(s32[256]{0:T(256)} %param.9) | copy-start | bytes 3076
  36.6 39.4 %copy-start.7 = (bf16[256,256]{1,0:T(8,128)(2,1)S(1)}, bf16[256,256]{1,0:T(8,128)(2,1)}, u32[]{:S(2)}) copy-start(bf16[256,256]{1,0:T(8,128)(2,1)} %constant.5.clone.frames_ref) | copy-start | bytes 393220

commit v4 on v3

--- a/solution.py
+++ b/solution.py
@@ -58,10 +58,12 @@
 
 
 def lane_order():
-    row = lax.broadcasted_iota(jnp.int32, (512, 512), 0)
-    column = lax.broadcasted_iota(jnp.int32, (512, 512), 1)
-    goal = ((row >> 5) & 3) * 128 + (row >> 7) * 32 + (row & 31)
-    return (goal == column).astype(F32).astype(BF)
+    m = np.zeros((512, 512), np.float32)
+    for fl in range(4):
+        for tl in range(4):
+            for i in range(32):
+                m[fl * 128 + tl * 32 + i, tl * 128 + fl * 32 + i] = 1
+    return m
 
 
 def frames_of(phase):
@@ -269,61 +271,53 @@
 
 
 def pair_kernel(
-    flag_ref, frames_ref, got_ref, weight_ref, vis, beam, y, vis_buf, beam_buf, sem, beam_sem
+    flag_ref, twice_ref, lanes_ref, frames_ref, got_ref, weight_ref, vis, beam, y, vis_buf, beam_buf, sem, beam_sem
 ):
     dot = functools.partial(jnp.dot, preferred_element_type=F32)
     dot_t = lambda a, b: lax.dot_general(a, b, (((1,), (1,)), ((), ())), preferred_element_type=F32)
-    lanes = lane_order()
-    station = lax.broadcasted_iota(jnp.int32, (INPUTS // 2, INPUTS), 0)
-    twice = (station == lax.broadcasted_iota(jnp.int32, (INPUTS // 2, INPUTS), 1) >> 1).astype(F32).astype(BF)
     used = jnp.broadcast_to(flag_ref[...].astype(F32), (8, INPUTS // 2)).astype(BF)
-    flags = dot(used, twice)[0:1]
+    flags = dot(used, twice_ref[...])[0:1]
     for fh in range(4):
         parts = [got_ref[(fh * 4 + fl) * 8 : (fh * 4 + fl) * 8 + 8].reshape(512, 128) for fl in range(4)]
-        block = dot(jnp.concatenate(parts, 1), lanes)
+        block = dot(jnp.concatenate(parts, 1), lanes_ref[...])
         flag = flags[:, fh * 128 : (fh + 1) * 128]
         for tl in range(4):
             y[fh * 4 + tl] = block[:, tl * 128 : (tl + 1) * 128] * flag
-    copies = {}
+    def prepare(s):
+        rows = [pl.ds(r * 8 + s, 32, stride=16) for r in range(2)]
+        pieces = [[[y[fh * 4 + tl, at, :] for fh in range(4)] for tl in range(4)] for at in rows]
+        w = jnp.concatenate([jnp.concatenate([jnp.concatenate(p, 1) for p in half], 0) for half in pieces], 0).astype(BF)
+        return w, w.T
+
+    def finish(s, by):
+        b_re = by[:BEAMS, :128] - by[BEAMS:, 128:]
+        b_im = by[BEAMS:, :128] + by[:BEAMS, 128:]
+        both = jnp.concatenate([b_re, b_im], 1).astype(BF)
+        beam_buf[s] = dot_t(frames_ref[...], both).astype(BF).reshape(128, 2, BEAMS)
+        copy = pltpu.make_async_copy(beam_buf.at[s], beam.at[s], beam_sem.at[s])
+        copy.start()
+        return copy
+
+    copies = []
     for s in range(SLOTS):
-        b = s
-        z = [
-            jnp.concatenate(
-                [
-                    jnp.concatenate([y[fh * 4 + tl, pl.ds(r * 8 + s, 32, stride=16), :] for fh in range(4)], 1)
-                    for tl in range(4)
-                ],
-                0,
-            ).astype(BF)
-            for r in range(2)
-        ]
-        w = jnp.concatenate(z, 0)
-        wt = w.T
+        w, wt = prepare(s)
+        by = dot(weight_ref[s].reshape(2 * BEAMS, INPUTS), wt)
         vt = jnp.concatenate([wt[:, 128:], -wt[:, :128]], 1)
-        started = []
         for c, left in enumerate((wt, vt)):
-            vis_buf[b, c] = (dot(left, w) * (1.0 / 128)).astype(BF)
-            started.append(pltpu.make_async_copy(vis_buf.at[b, c], vis.at[s, c], sem.at[b, c]))
-            started[-1].start()
-        w_re, w_im = weight_ref[s, 0], weight_ref[s, 1]
-        by_re, by_im = dot_t(w, w_re), dot_t(w, w_im)
-        b_re = by_re[:128] - by_im[128:]
-        b_im = by_im[:128] + by_re[128:]
-        both = jnp.concatenate([b_re, b_im], 0).astype(BF)
-        beam_buf[b] = dot(frames_ref[...], both).astype(BF).reshape(128, 2, BEAMS)
-        started.append(pltpu.make_async_copy(beam_buf.at[b], beam.at[s], beam_sem.at[b]))
-        started[-1].start()
-        copies[s] = started
-    for started in copies.values():
-        for copy in started:
-            copy.wait()
+            vis_buf[s, c] = (dot(left, w) * (1.0 / 128)).astype(BF)
+            copies.append(pltpu.make_async_copy(vis_buf.at[s, c], vis.at[s, c], sem.at[s, c]))
+            copies[-1].start()
+        copies.append(finish(s, by))
+    for copy in copies:
+        copy.wait()
 
 
 def make_outputs(flags, got, weights):
-    frames = jnp.asarray(frame_order(), BF)
+    twice = np.repeat(np.eye(INPUTS // 2), 2, 1)
+    consts = [jnp.asarray(m, BF) for m in (twice, lane_order(), frame_order())]
     return pl.pallas_call(
         pair_kernel,
-        in_specs=[VM] * 4,
+        in_specs=[VM] * 6,
         out_specs=[ANY, ANY],
         out_shape=[
             jax.ShapeDtypeStruct((SLOTS, 2, INPUTS, INPUTS), BF),
@@ -339,7 +333,7 @@
         compiler_params=pltpu.CompilerParams(vmem_limit_bytes=20 * MIB),
         cost_estimate=pl.CostEstimate(flops=5_000_000_000, transcendentals=0, bytes_accessed=16 * MIB),
         name="pairs",
-    )(flags, frames, got, weights)
+    )(flags, *consts, got, weights)
 
 
 def shards(voltages, station_flags, owner_map, beam_table, table_gains, table_delays):

time: 85.3 us -> 83.2 us (0.975)
  Pallas kernels: 32.7 us -> 30.6 us
    pallas_call x1, Pallas kernels: 8.94 us -> 6.79 us  [make_outputs(): pl.pallas_call(pair_kernel, in_specs=[VM] * 6, out_specs=[ANY, ANY], out_...]
where the time goes in v4:
time: 83.2 us; the launch traced here: 83.1 us
  blocking collectives  39.4 us (47%)
  Pallas kernels  30.6 us (37%)
  starting transfers between devices  11.1 us (13%)
  between operations  0.98 us (1%)
  waiting for transfers between devices  0.93 us (1%)
    all_to_all x1, blocking collectives, shards(): lax.all_to_all(spectra, ('freq', 'tm'), split_axis=0, concat_axis=0, tile...  39.4 us
    pallas_call x2, Pallas kernels, make_spectra(): pl.pallas_call(functools.partial(spectra_kernel, phase), in_specs=[VM] *...  11.5 us
    ppermute x2, starting transfers between devices, shards(): lax.ppermute(x, 'tm', [(i, (i - 1) % n_time) for i in range(n_time)])  11.1 us
    pallas_call x1, Pallas kernels, make_weights(): pl.pallas_call(weight_kernel, in_specs=[SM, SM, VM, VM], out_specs=VM, ou...  6.82 us
    pallas_call x1, Pallas kernels, make_outputs(): pl.pallas_call(pair_kernel, in_specs=[VM] * 6, out_specs=[ANY, ANY], out_...  6.79 us
    pallas_call x1, Pallas kernels, make_table(): pl.pallas_call(table_kernel, in_specs=[VM], out_specs=[VM, VM], out_shape...  3.89 us
  transfers between devices with their start and end apart: 4, of which 1 were waited for; matrix products, arithmetic and copies ran while one was open for 0% of the time, Pallas kernels for 22%

profile of v4, /device:TPU:1, one launch (start us, length us, event | category | flops | bytes accessed | tf_op | source)
XLA Modules:
  0.0 83.1 jit_solution(13260819990905232166)
XLA Ops:
  0.7 1.6 %cut.1 = (bf16[32,8192]{1,0:T(8,128)(2,1)S(1)}, bf16[32,6144]{1,0:T(8,128)(2,1)S(1)}, bf16[32,8192]{1,0:T(8,128)(2,1)S(1)}, bf16[32,8192]{1,0:T(8,128)(2,1)S(1)}) custom-call(bf16[32,32768]{1,0:T(8,128)(2,1)} %refs_0_.1), custom_call_target="tpu_custom_call" | custom-call | bytes 2097152 | tf_op jit(solution)/shard_map/cut/pallas_call | solution.py:173
  2.3 6.0 %collective-permute-start.3 = (bf16[32,8192]{1,0:T(8,128)(2,1)S(1)}, bf16[32,8192]{1,0:T(8,128)(2,1)S(1)}, u32[]{:S(2)}, u32[]{:S(2)}) collective-permute-start(bf16[32,8192]{1,0:T(8,128)(2,1)S(1)} %get-tuple-element.15), channel_id=1, source_target_pairs={{0,112},{16,0},{32,16},{48,32},{64,48},{80,64},{96,80},{112,96},{1... | collective-permute-start | bytes 1572872 | tf_op jit(solution)/shard_map/ppermute | solution.py:342
  8.3 0.0 collective-permute-start.2
  8.3 0.0 collective-permute-start
  8.3 5.1 %collective-permute-start.1 = (bf16[32,8192]{1,0:T(8,128)(2,1)S(1)}, bf16[32,8192]{1,0:T(8,128)(2,1)S(1)}, u32[]{:S(2)}, u32[]{:S(2)}) collective-permute-start(bf16[32,8192]{1,0:T(8,128)(2,1)S(1)} %get-tuple-element.11), channel_id=1, source_target_pairs={{0,112},{16,0},{32,16},{48,32},{64,48},{80,64},{96,80},{112,96},{1... | collective-permute-start | bytes 1572872 | tf_op jit(solution)/shard_map/ppermute | solution.py:342
  13.4 3.9 %table.1 = (bf16[1024,2048]{1,0:T(8,128)(2,1)S(1)}, bf16[1024,2048]{1,0:T(8,128)(2,1)S(1)}) custom-call(s32[8,128]{1,0:T(8,128)S(1)} %bitcast.2), custom_call_target="tpu_custom_call" | custom-call | flops 33554432 | bytes 8388608 | tf_op jit(solution)/shard_map/table/pallas_call | solution.py:110
  17.3 0.0 copy-done.3
  17.3 0.0 copy-done.2
  17.3 0.0 copy-done.5
  17.3 0.0 copy-start
  17.3 0.0 copy-start.1
  17.4 6.8 %weights.1.refs_6_.weight_ref = bf16[8,2,256,512]{3,2,1,0:T(8,128)(2,1)S(1)} custom-call(s32[1024]{0:T(1024)S(1)} %copy-done.4, s32[256]{0:T(256)S(1)} %copy-done.5, f32[256,512]{1,0:T(8,128)S(1)} %copy-done.2, f32[256,512]{1,0:T(8,128)S(1)} %copy-done.3), custom_call_target="tpu_custom_call" | custom-call | flops 52428800 | bytes 6291456 | tf_op jit(solution)/shard_map/weights/pallas_call | solution.py:148
  24.2 0.0 collective-permute-done.2.refs_1_
  24.2 0.0 collective-permute-done.3.refs_2_
  24.2 7.7 %spectra0.1 = (bf16[128,64,128]{2,1,0:T(8,128)(2,1)S(1)}, f32[256,2048]{1,0:T(8,128)S(1)}) custom-call(bf16[32,32768]{1,0:T(8,128)(2,1)S(1)} %copy-done, bf16[32,6144]{1,0:T(8,128)(2,1)S(1)} %collective-permute-done.2.refs_1_, bf16[32,8192]{1,0:T(8,128)(2,1)S(1)} %collective-permute-done.3.refs_2_, f32[16,2048]{1,0:T(8,128)S(1)} %copy-done.1, ...), custom_call_target="tpu_custom_call" | custom-call | flops 2147483648 | bytes 12582912 | tf_op jit(solution)/shard_map/spectra0/pallas_call | solution.py:256
  31.9 0.9 %collective-permute-done.refs_0_ = bf16[32,8192]{1,0:T(8,128)(2,1)S(1)} collective-permute-done((bf16[32,8192]{1,0:T(8,128)(2,1)S(1)}, bf16[32,8192]{1,0:T(8,128)(2,1)S(1)}, u32[]{:S(2)}, u32[]{:S(2)}) %collective-permute-start) | collective-permute-done | bytes 524320 | tf_op jit(solution)/shard_map/ppermute | solution.py:341
  32.8 0.0 collective-permute-done.1.refs_1_
  32.8 3.8 %spectra1.1 = bf16[128,64,128]{2,1,0:T(8,128)(2,1)S(1)} custom-call(bf16[32,8192]{1,0:T(8,128)(2,1)S(1)} %collective-permute-done.refs_0_, bf16[32,8192]{1,0:T(8,128)(2,1)S(1)} %collective-permute-done.1.refs_1_, f32[16,2048]{1,0:T(8,128)S(1)} %copy-done.1, bf16[1024,2048]{1,0:T(8,128)(2,1)S(1)} %get-tuple-element.12.refs_4_.refs_3_, ...), custom_call_target="tpu_custom_call", output_to_operand_aliasing={{}: (6, {})} | custom-call | flops 2147483648 | bytes 12582912 | tf_op jit(solution)/shard_map/spectra1/pallas_call | solution.py:256
  36.6 0.0 copy-start.6
  36.6 0.0 copy-start.7
  36.7 0.0 copy-start.8
  36.7 0.0 copy-start.9
  36.7 39.4 %all_to_all.5.got_ref = bf16[128,64,128]{2,1,0:T(8,128)(2,1)S(1)} all-to-all(bf16[128,64,128]{2,1,0:T(8,128)(2,1)S(1)} %spectra1.1), channel_id=1, replica_groups=mesh['tm'=8,'freq'=16] {'freq','tm'}, dimensions={0} | all-to-all | bytes 4194304 | tf_op jit(solution)/shard_map/all_to_all | solution.py:352
  76.1 6.8 %pairs.1 = (bf16[8,2,512,512]{3,2,1,0:T(8,128)(2,1)}, bf16[8,128,2,256]{3,2,1,0:T(2,128)(2,1)}) custom-call(s32[1,256]{1,0:T(1,128)S(1)} %bitcast.3, bf16[256,512]{1,0:T(8,128)(2,1)S(1)} %copy-done.8, bf16[512,512]{1,0:T(8,128)(2,1)S(1)} %copy-done.7, bf16[256,256]{1,0:T(8,128)(2,1)S(1)} %copy-done.9, bf16[128,64,128]{2,1,0:T(8,128)(2,1)S(1)} %all_to_all.5.got_ref, ...), custom_call_target="tpu_custom_call" | custom-call | flops 5000000000 | bytes 16777216 | tf_op jit(solution)/shard_map/pairs/pallas_call | solution.py:318
  (11 shorter events, 0.0 us)
Async XLA Ops:
  0.6 12.8 %copy-start.4 = (s32[1024]{0:T(1024)S(1)}, s32[1024]{0:T(1024)}, u32[]{:S(2)}) copy-start(s32[1024]{0:T(1024)} %owner_ref.1) | copy-start | bytes 12292
  0.6 16.7 %copy-start.3 = (f32[256,512]{1,0:T(8,128)S(1)}, f32[256,512]{1,0:T(8,128)}, u32[]{:S(2)}) copy-start(f32[256,512]{1,0:T(8,128)} %delays_ref.1) | copy-start | bytes 1572868
  0.7 16.7 %copy-start.2 = (f32[256,512]{1,0:T(8,128)S(1)}, f32[256,512]{1,0:T(8,128)}, u32[]{:S(2)}) copy-start(f32[256,512]{1,0:T(8,128)} %gains_ref.1) | copy-start | bytes 1572868
  0.7 16.7 %copy-start.5 = (s32[256]{0:T(256)S(1)}, s32[256]{0:T(256)}, u32[]{:S(2)}) copy-start(s32[256]{0:T(256)} %beam_ref.1) | copy-start | bytes 3076
  2.3 21.9 %collective-permute-start.3 = (bf16[32,8192]{1,0:T(8,128)(2,1)S(1)}, bf16[32,8192]{1,0:T(8,128)(2,1)S(1)}, u32[]{:S(2)}, u32[]{:S(2)}) collective-permute-start(bf16[32,8192]{1,0:T(8,128)(2,1)S(1)} %get-tuple-element.15), channel_id=1, source_target_pairs={{0,112},{16,0},{32,16},{48,32},{64,48},{80,64},{96,80},{112,96},{1... | collective-permute-start | bytes 1572872 | tf_op jit(solution)/shard_map/ppermute | solution.py:342
  8.3 15.9 %collective-permute-start.2 = (bf16[32,6144]{1,0:T(8,128)(2,1)S(1)}, bf16[32,6144]{1,0:T(8,128)(2,1)S(1)}, u32[]{:S(2)}, u32[]{:S(2)}) collective-permute-start(bf16[32,6144]{1,0:T(8,128)(2,1)S(1)} %get-tuple-element.14), channel_id=1, source_target_pairs={{0,16},{16,32},{32,48},{48,64},{64,80},{80,96},{96,112},{112,0},{1... | collective-permute-start | bytes 1179656 | tf_op jit(solution)/shard_map/ppermute | solution.py:341
  8.3 24.5 %collective-permute-start = (bf16[32,8192]{1,0:T(8,128)(2,1)S(1)}, bf16[32,8192]{1,0:T(8,128)(2,1)S(1)}, u32[]{:S(2)}, u32[]{:S(2)}) collective-permute-start(bf16[32,8192]{1,0:T(8,128)(2,1)S(1)} %get-tuple-element.10), channel_id=1, source_target_pairs={{0,16},{16,32},{32,48},{48,64},{64,80},{80,96},{96,112},{112,0},{1... | collective-permute-start | bytes 1572872 | tf_op jit(solution)/shard_map/ppermute | solution.py:341
  8.3 24.5 %collective-permute-start.1 = (bf16[32,8192]{1,0:T(8,128)(2,1)S(1)}, bf16[32,8192]{1,0:T(8,128)(2,1)S(1)}, u32[]{:S(2)}, u32[]{:S(2)}) collective-permute-start(bf16[32,8192]{1,0:T(8,128)(2,1)S(1)} %get-tuple-element.11), channel_id=1, source_target_pairs={{0,112},{16,0},{32,16},{48,32},{64,48},{80,64},{96,80},{112,96},{1... | collective-permute-start | bytes 1572872 | tf_op jit(solution)/shard_map/ppermute | solution.py:342
  17.3 6.9 %copy-start = (bf16[32,32768]{1,0:T(8,128)(2,1)S(1)}, bf16[32,32768]{1,0:T(8,128)(2,1)}, u32[]{:S(2)}) copy-start(bf16[32,32768]{1,0:T(8,128)(2,1)} %refs_0_.1) | copy-start | bytes 6291460
  17.3 6.9 %copy-start.1 = (f32[16,2048]{1,0:T(8,128)S(1)}, f32[16,2048]{1,0:T(8,128)}, u32[]{:S(2)}) copy-start(f32[16,2048]{1,0:T(8,128)} %constant.8.clone.refs_3_.refs_2_) | copy-start | bytes 393220
  36.6 39.5 %copy-start.6 = (s32[256]{0:T(256)S(1)}, s32[256]{0:T(256)}, u32[]{:S(2)}) copy-start(s32[256]{0:T(256)} %param.11) | copy-start | bytes 3076
  36.6 39.4 %copy-start.7 = (bf16[512,512]{1,0:T(8,128)(2,1)S(1)}, bf16[512,512]{1,0:T(8,128)(2,1)}, u32[]{:S(2)}) copy-start(bf16[512,512]{1,0:T(8,128)(2,1)} %constant.10.clone.lanes_ref) | copy-start | bytes 1572868
  36.7 39.4 %copy-start.8 = (bf16[256,512]{1,0:T(8,128)(2,1)S(1)}, bf16[256,512]{1,0:T(8,128)(2,1)}, u32[]{:S(2)}) copy-start(bf16[256,512]{1,0:T(8,128)(2,1)} %constant.9.clone.twice_ref) | copy-start | bytes 786436
  36.7 39.4 %copy-start.9 = (bf16[256,256]{1,0:T(8,128)(2,1)S(1)}, bf16[256,256]{1,0:T(8,128)(2,1)}, u32[]{:S(2)}) copy-start(bf16[256,256]{1,0:T(8,128)(2,1)} %constant.11.clone.frames_ref) | copy-start | bytes 393220

commit v5 on v4

--- a/solution.py
+++ b/solution.py
@@ -184,10 +184,10 @@
 
 def spectra_kernel(phase, *refs):
     if phase == 0:
-        own, p1, n1, taps_ref, cos_ref, sin_ref, *_, out, held, filt, message, sem = refs
+        own, p1, n1, taps_ref, cos_ref, sin_ref, *_, out, held, filt = refs
         p2 = n2 = None
     else:
-        p2, n2, taps_ref, cos_ref, sin_ref, held, *_, out, filt, message, sem = refs
+        p2, n2, taps_ref, cos_ref, sin_ref, held, *_, out, filt = refs
         own = p1 = n1 = None
     pieces = [(p2, f) for f in range(4)] + [(p1, f) for f in range(3)] + [(own, f) for f in range(FR)]
     pieces += [(n1, f) for f in range(4)] + [(n2, f) for f in range(4)]
@@ -231,22 +231,17 @@
         return carry
 
     lax.fori_loop(0, L // 128, column, 0)
-    copies = []
-    for q in range(4):
-        rows = slice(q * 256, q * 256 + 256)
+    for q in range(2):
+        rows = slice(q * 512, q * 512 + 512)
         dot = lambda ref: lax.dot_general(
             ref[rows, :], filt[...], (((1,), (1,)), ((), ())), preferred_element_type=F32
         ) * (1.0 / math.sqrt(L))
         re, im = dot(cos_ref), dot(sin_ref)
         for th in range(2):
             lanes = slice(th * 128, th * 128 + 128)
-            both = [re[:, lanes].reshape(32, SLOTS, 128), im[:, lanes].reshape(32, SLOTS, 128)]
-            message[q * 32 : q * 32 + 32, th * 16 : th * 16 + 16, :] = jnp.concatenate(both, 1).astype(BF)
-        at = pl.ds(q * 32, 32)
-        copies.append(pltpu.make_async_copy(message.at[at], out.at[at, pl.ds(phase * 32, 32)], sem.at[q]))
-        copies[-1].start()
-    for copy in copies:
-        copy.wait()
+            both = [re[:, lanes].reshape(64, SLOTS, 128), im[:, lanes].reshape(64, SLOTS, 128)]
+            at = phase * 32 + th * 16
+            out[q * 64 : q * 64 + 64, at : at + 16, :] = jnp.concatenate(both, 1).astype(BF)
 
 
 def make_spectra(phase, args, after=()):
@@ -255,15 +250,11 @@
     out = pltpu.VMEM((128, 64, 128), BF)
     return pl.pallas_call(
         functools.partial(spectra_kernel, phase),
-        in_specs=[VM] * ready + [ANY] * len(after),
-        out_specs=ANY if phase else [ANY, VM],
+        in_specs=[VM] * ready + [VM if phase else ANY] * len(after),
+        out_specs=VM if phase else [VM, VM],
         out_shape=out if phase else [out, pltpu.VMEM((8 * IN_DEV, L), F32)],
         input_output_aliases={len(args) - 1: 0} if phase else {},
-        scratch_shapes=[
-            pltpu.VMEM((8 * IN_DEV, L), BF),
-            pltpu.VMEM((128, 32, 128), BF),
-            pltpu.SemaphoreType.DMA((4,)),
-        ],
+        scratch_shapes=[pltpu.VMEM((8 * IN_DEV, L), BF)],
         compiler_params=pltpu.CompilerParams(vmem_limit_bytes=8 * MIB),
         cost_estimate=pl.CostEstimate(flops=4 * CH * L * 256, transcendentals=0, bytes_accessed=12 * MIB),
         name="spectra%d" % phase,

time: 83.2 us -> 82.5 us (level)
  Pallas kernels: 30.6 us -> 29.1 us
    pallas_call x2, Pallas kernels: 11.5 us -> 9.96 us  [make_spectra(): pl.pallas_call(functools.partial(spectra_kernel, phase), in_specs=[VM] *...]
  transfers between devices with their start and end apart: 4 -> 4, of which waited for: 1 -> 1; matrix products, arithmetic and copies ran while one was open for 0% -> 0% of each run, Pallas kernels for 22% -> 21%
where the time goes in v5:
time: 82.5 us; the launch traced here: 82.3 us
  blocking collectives  39.4 us (48%)
  Pallas kernels  29.1 us (35%)
  starting transfers between devices  11.1 us (13%)
  waiting for transfers between devices  1.68 us (2%)
  between operations  0.98 us (1%)
    all_to_all x1, blocking collectives, shards(): lax.all_to_all(spectra, ('freq', 'tm'), split_axis=0, concat_axis=0, tile...  39.4 us
    ppermute x2, starting transfers between devices, shards(): lax.ppermute(x, 'tm', [(i, (i - 1) % n_time) for i in range(n_time)])  11.1 us
    pallas_call x2, Pallas kernels, make_spectra(): pl.pallas_call(functools.partial(spectra_kernel, phase), in_specs=[VM] *...  9.96 us
    pallas_call x1, Pallas kernels, make_weights(): pl.pallas_call(weight_kernel, in_specs=[SM, SM, VM, VM], out_specs=VM, ou...  6.82 us
    pallas_call x1, Pallas kernels, make_outputs(): pl.pallas_call(pair_kernel, in_specs=[VM] * 6, out_specs=[ANY, ANY], out_...  6.79 us
    pallas_call x1, Pallas kernels, make_table(): pl.pallas_call(table_kernel, in_specs=[VM], out_specs=[VM, VM], out_shape...  3.89 us
    ppermute x2, waiting for transfers between devices, shards(): lax.ppermute(x, 'tm', [(i, (i + 1) % n_time) for i in range(n_time)])  1.68 us
  transfers between devices with their start and end apart: 4, of which 1 were waited for; matrix products, arithmetic and copies ran while one was open for 0% of the time, Pallas kernels for 21%

profile of v5, /device:TPU:1, one launch (start us, length us, event | category | flops | bytes accessed | tf_op | source)
XLA Modules:
  0.0 82.3 jit_solution(15193527011026587321)
XLA Ops:
  0.7 1.6 %cut.1 = (bf16[32,8192]{1,0:T(8,128)(2,1)S(1)}, bf16[32,6144]{1,0:T(8,128)(2,1)S(1)}, bf16[32,8192]{1,0:T(8,128)(2,1)S(1)}, bf16[32,8192]{1,0:T(8,128)(2,1)S(1)}) custom-call(bf16[32,32768]{1,0:T(8,128)(2,1)} %refs_0_.1), custom_call_target="tpu_custom_call" | custom-call | bytes 2097152 | tf_op jit(solution)/shard_map/cut/pallas_call | solution.py:173
  2.3 6.0 %collective-permute-start.3 = (bf16[32,8192]{1,0:T(8,128)(2,1)S(1)}, bf16[32,8192]{1,0:T(8,128)(2,1)S(1)}, u32[]{:S(2)}, u32[]{:S(2)}) collective-permute-start(bf16[32,8192]{1,0:T(8,128)(2,1)S(1)} %get-tuple-element.15), channel_id=1, source_target_pairs={{0,112},{16,0},{32,16},{48,32},{64,48},{80,64},{96,80},{112,96},{1... | collective-permute-start | bytes 1572872 | tf_op jit(solution)/shard_map/ppermute | solution.py:333
  8.3 0.0 collective-permute-start.2
  8.3 0.0 collective-permute-start
  8.3 5.1 %collective-permute-start.1 = (bf16[32,8192]{1,0:T(8,128)(2,1)S(1)}, bf16[32,8192]{1,0:T(8,128)(2,1)S(1)}, u32[]{:S(2)}, u32[]{:S(2)}) collective-permute-start(bf16[32,8192]{1,0:T(8,128)(2,1)S(1)} %get-tuple-element.11), channel_id=1, source_target_pairs={{0,112},{16,0},{32,16},{48,32},{64,48},{80,64},{96,80},{112,96},{1... | collective-permute-start | bytes 1572872 | tf_op jit(solution)/shard_map/ppermute | solution.py:333
  13.4 3.9 %table.1 = (bf16[1024,2048]{1,0:T(8,128)(2,1)S(1)}, bf16[1024,2048]{1,0:T(8,128)(2,1)S(1)}) custom-call(s32[8,128]{1,0:T(8,128)S(1)} %bitcast.2), custom_call_target="tpu_custom_call" | custom-call | flops 33554432 | bytes 8388608 | tf_op jit(solution)/shard_map/table/pallas_call | solution.py:110
  17.3 0.0 copy-done.3
  17.3 0.0 copy-done.2
  17.3 0.0 copy-done.5
  17.3 0.0 copy-start
  17.3 0.0 copy-start.1
  17.4 6.8 %weights.1.refs_6_.weight_ref = bf16[8,2,256,512]{3,2,1,0:T(8,128)(2,1)S(1)} custom-call(s32[1024]{0:T(1024)S(1)} %copy-done.4, s32[256]{0:T(256)S(1)} %copy-done.5, f32[256,512]{1,0:T(8,128)S(1)} %copy-done.2, f32[256,512]{1,0:T(8,128)S(1)} %copy-done.3), custom_call_target="tpu_custom_call" | custom-call | flops 52428800 | bytes 6291456 | tf_op jit(solution)/shard_map/weights/pallas_call | solution.py:148
  24.2 0.0 collective-permute-done.2.refs_1_
  24.2 0.0 collective-permute-done.3.refs_2_
  24.2 6.9 %spectra0.1 = (bf16[128,64,128]{2,1,0:T(8,128)(2,1)S(1)}, f32[256,2048]{1,0:T(8,128)S(1)}) custom-call(bf16[32,32768]{1,0:T(8,128)(2,1)S(1)} %copy-done, bf16[32,6144]{1,0:T(8,128)(2,1)S(1)} %collective-permute-done.2.refs_1_, bf16[32,8192]{1,0:T(8,128)(2,1)S(1)} %collective-permute-done.3.refs_2_, f32[16,2048]{1,0:T(8,128)S(1)} %copy-done.1, ...), custom_call_target="tpu_custom_call" | custom-call | flops 2147483648 | bytes 12582912 | tf_op jit(solution)/shard_map/spectra0/pallas_call | solution.py:251
  31.1 1.7 %collective-permute-done.refs_0_ = bf16[32,8192]{1,0:T(8,128)(2,1)S(1)} collective-permute-done((bf16[32,8192]{1,0:T(8,128)(2,1)S(1)}, bf16[32,8192]{1,0:T(8,128)(2,1)S(1)}, u32[]{:S(2)}, u32[]{:S(2)}) %collective-permute-start) | collective-permute-done | bytes 524320 | tf_op jit(solution)/shard_map/ppermute | solution.py:332
  32.8 0.0 collective-permute-done.1.refs_1_
  32.8 3.1 %spectra1.1 = bf16[128,64,128]{2,1,0:T(8,128)(2,1)S(1)} custom-call(bf16[32,8192]{1,0:T(8,128)(2,1)S(1)} %collective-permute-done.refs_0_, bf16[32,8192]{1,0:T(8,128)(2,1)S(1)} %collective-permute-done.1.refs_1_, f32[16,2048]{1,0:T(8,128)S(1)} %copy-done.1, bf16[1024,2048]{1,0:T(8,128)(2,1)S(1)} %get-tuple-element.12.refs_4_.refs_3_, ...), custom_call_target="tpu_custom_call", output_to_operand_aliasing={{}: (6, {})} | custom-call | flops 2147483648 | bytes 12582912 | tf_op jit(solution)/shard_map/spectra1/pallas_call | solution.py:251
  35.9 0.0 copy-start.6
  35.9 0.0 copy-start.7
  35.9 0.0 copy-start.8
  35.9 0.0 copy-start.9
  35.9 39.4 %all_to_all.5.got_ref = bf16[128,64,128]{2,1,0:T(8,128)(2,1)S(1)} all-to-all(bf16[128,64,128]{2,1,0:T(8,128)(2,1)S(1)} %spectra1.1), channel_id=1, replica_groups=mesh['tm'=8,'freq'=16] {'freq','tm'}, dimensions={0} | all-to-all | bytes 4194304 | tf_op jit(solution)/shard_map/all_to_all | solution.py:343
  75.4 6.8 %pairs.1 = (bf16[8,2,512,512]{3,2,1,0:T(8,128)(2,1)}, bf16[8,128,2,256]{3,2,1,0:T(2,128)(2,1)}) custom-call(s32[1,256]{1,0:T(1,128)S(1)} %bitcast.3, bf16[256,512]{1,0:T(8,128)(2,1)S(1)} %copy-done.8, bf16[512,512]{1,0:T(8,128)(2,1)S(1)} %copy-done.7, bf16[256,256]{1,0:T(8,128)(2,1)S(1)} %copy-done.9, bf16[128,64,128]{2,1,0:T(8,128)(2,1)S(1)} %all_to_all.5.got_ref, ...), custom_call_target="tpu_custom_call" | custom-call | flops 5000000000 | bytes 16777216 | tf_op jit(solution)/shard_map/pairs/pallas_call | solution.py:309
  (11 shorter events, 0.0 us)
Async XLA Ops:
  0.6 12.8 %copy-start.4 = (s32[1024]{0:T(1024)S(1)}, s32[1024]{0:T(1024)}, u32[]{:S(2)}) copy-start(s32[1024]{0:T(1024)} %owner_ref.1) | copy-start | bytes 12292
  0.6 16.7 %copy-start.3 = (f32[256,512]{1,0:T(8,128)S(1)}, f32[256,512]{1,0:T(8,128)}, u32[]{:S(2)}) copy-start(f32[256,512]{1,0:T(8,128)} %delays_ref.1) | copy-start | bytes 1572868
  0.7 16.7 %copy-start.2 = (f32[256,512]{1,0:T(8,128)S(1)}, f32[256,512]{1,0:T(8,128)}, u32[]{:S(2)}) copy-start(f32[256,512]{1,0:T(8,128)} %gains_ref.1) | copy-start | bytes 1572868
  0.7 16.7 %copy-start.5 = (s32[256]{0:T(256)S(1)}, s32[256]{0:T(256)}, u32[]{:S(2)}) copy-start(s32[256]{0:T(256)} %beam_ref.1) | copy-start | bytes 3076
  2.3 21.9 %collective-permute-start.3 = (bf16[32,8192]{1,0:T(8,128)(2,1)S(1)}, bf16[32,8192]{1,0:T(8,128)(2,1)S(1)}, u32[]{:S(2)}, u32[]{:S(2)}) collective-permute-start(bf16[32,8192]{1,0:T(8,128)(2,1)S(1)} %get-tuple-element.15), channel_id=1, source_target_pairs={{0,112},{16,0},{32,16},{48,32},{64,48},{80,64},{96,80},{112,96},{1... | collective-permute-start | bytes 1572872 | tf_op jit(solution)/shard_map/ppermute | solution.py:333
  8.3 15.9 %collective-permute-start.2 = (bf16[32,6144]{1,0:T(8,128)(2,1)S(1)}, bf16[32,6144]{1,0:T(8,128)(2,1)S(1)}, u32[]{:S(2)}, u32[]{:S(2)}) collective-permute-start(bf16[32,6144]{1,0:T(8,128)(2,1)S(1)} %get-tuple-element.14), channel_id=1, source_target_pairs={{0,16},{16,32},{32,48},{48,64},{64,80},{80,96},{96,112},{112,0},{1... | collective-permute-start | bytes 1179656 | tf_op jit(solution)/shard_map/ppermute | solution.py:332
  8.3 24.5 %collective-permute-start = (bf16[32,8192]{1,0:T(8,128)(2,1)S(1)}, bf16[32,8192]{1,0:T(8,128)(2,1)S(1)}, u32[]{:S(2)}, u32[]{:S(2)}) collective-permute-start(bf16[32,8192]{1,0:T(8,128)(2,1)S(1)} %get-tuple-element.10), channel_id=1, source_target_pairs={{0,16},{16,32},{32,48},{48,64},{64,80},{80,96},{96,112},{112,0},{1... | collective-permute-start | bytes 1572872 | tf_op jit(solution)/shard_map/ppermute | solution.py:332
  8.3 24.5 %collective-permute-start.1 = (bf16[32,8192]{1,0:T(8,128)(2,1)S(1)}, bf16[32,8192]{1,0:T(8,128)(2,1)S(1)}, u32[]{:S(2)}, u32[]{:S(2)}) collective-permute-start(bf16[32,8192]{1,0:T(8,128)(2,1)S(1)} %get-tuple-element.11), channel_id=1, source_target_pairs={{0,112},{16,0},{32,16},{48,32},{64,48},{80,64},{96,80},{112,96},{1... | collective-permute-start | bytes 1572872 | tf_op jit(solution)/shard_map/ppermute | solution.py:333
  17.3 6.9 %copy-start = (bf16[32,32768]{1,0:T(8,128)(2,1)S(1)}, bf16[32,32768]{1,0:T(8,128)(2,1)}, u32[]{:S(2)}) copy-start(bf16[32,32768]{1,0:T(8,128)(2,1)} %refs_0_.1) | copy-start | bytes 6291460
  17.3 6.9 %copy-start.1 = (f32[16,2048]{1,0:T(8,128)S(1)}, f32[16,2048]{1,0:T(8,128)}, u32[]{:S(2)}) copy-start(f32[16,2048]{1,0:T(8,128)} %constant.8.clone.refs_3_.refs_2_) | copy-start | bytes 393220
  35.9 39.5 %copy-start.6 = (s32[256]{0:T(256)S(1)}, s32[256]{0:T(256)}, u32[]{:S(2)}) copy-start(s32[256]{0:T(256)} %param.11) | copy-start | bytes 3076
  35.9 39.5 %copy-start.7 = (bf16[512,512]{1,0:T(8,128)(2,1)S(1)}, bf16[512,512]{1,0:T(8,128)(2,1)}, u32[]{:S(2)}) copy-start(bf16[512,512]{1,0:T(8,128)(2,1)} %constant.10.clone.lanes_ref) | copy-start | bytes 1572868
  35.9 39.5 %copy-start.8 = (bf16[256,512]{1,0:T(8,128)(2,1)S(1)}, bf16[256,512]{1,0:T(8,128)(2,1)}, u32[]{:S(2)}) copy-start(bf16[256,512]{1,0:T(8,128)(2,1)} %constant.9.clone.twice_ref) | copy-start | bytes 786436
  35.9 39.4 %copy-start.9 = (bf16[256,256]{1,0:T(8,128)(2,1)S(1)}, bf16[256,256]{1,0:T(8,128)(2,1)}, u32[]{:S(2)}) copy-start(bf16[256,256]{1,0:T(8,128)(2,1)} %constant.11.clone.frames_ref) | copy-start | bytes 393220

commit v6 on v5

--- a/solution.py
+++ b/solution.py
@@ -231,17 +231,17 @@
         return carry
 
     lax.fori_loop(0, L // 128, column, 0)
-    for q in range(2):
-        rows = slice(q * 512, q * 512 + 512)
+    for q in range(1):
+        rows = slice(q * 1024, q * 1024 + 1024)
         dot = lambda ref: lax.dot_general(
             ref[rows, :], filt[...], (((1,), (1,)), ((), ())), preferred_element_type=F32
         ) * (1.0 / math.sqrt(L))
         re, im = dot(cos_ref), dot(sin_ref)
         for th in range(2):
             lanes = slice(th * 128, th * 128 + 128)
-            both = [re[:, lanes].reshape(64, SLOTS, 128), im[:, lanes].reshape(64, SLOTS, 128)]
+            both = [re[:, lanes].reshape(128, SLOTS, 128), im[:, lanes].reshape(128, SLOTS, 128)]
             at = phase * 32 + th * 16
-            out[q * 64 : q * 64 + 64, at : at + 16, :] = jnp.concatenate(both, 1).astype(BF)
+            out[q * 128 : q * 128 + 128, at : at + 16, :] = jnp.concatenate(both, 1).astype(BF)
 
 
 def make_spectra(phase, args, after=()):

time: 82.5 us -> 82.5 us (level)
  no operation moved by 1% of the time
where the time goes in v6:
time: 82.5 us; the launch traced here: 82.3 us
  blocking collectives  39.4 us (48%)
  Pallas kernels  29 us (35%)
  starting transfers between devices  11.1 us (13%)
  waiting for transfers between devices  1.69 us (2%)
  between operations  0.98 us (1%)
    all_to_all x1, blocking collectives, shards(): lax.all_to_all(spectra, ('freq', 'tm'), split_axis=0, concat_axis=0, tile...  39.4 us
    ppermute x2, starting transfers between devices, shards(): lax.ppermute(x, 'tm', [(i, (i - 1) % n_time) for i in range(n_time)])  11.1 us
    pallas_call x2, Pallas kernels, make_spectra(): pl.pallas_call(functools.partial(spectra_kernel, phase), in_specs=[VM] *...  9.94 us
    pallas_call x1, Pallas kernels, make_weights(): pl.pallas_call(weight_kernel, in_specs=[SM, SM, VM, VM], out_specs=VM, ou...  6.82 us
    pallas_call x1, Pallas kernels, make_outputs(): pl.pallas_call(pair_kernel, in_specs=[VM] * 6, out_specs=[ANY, ANY], out_...  6.79 us
    pallas_call x1, Pallas kernels, make_table(): pl.pallas_call(table_kernel, in_specs=[VM], out_specs=[VM, VM], out_shape...  3.89 us
    ppermute x2, waiting for transfers between devices, shards(): lax.ppermute(x, 'tm', [(i, (i + 1) % n_time) for i in range(n_time)])  1.68 us
  transfers between devices with their start and end apart: 4, of which 1 were waited for; matrix products, arithmetic and copies ran while one was open for 0% of the time, Pallas kernels for 21%

profile of v6, /device:TPU:1, one launch (start us, length us, event | category | flops | bytes accessed | tf_op | source)
XLA Modules:
  0.0 82.3 jit_solution(15655159375053286847)
XLA Ops:
  0.6 0.0 copy-start.4
  0.7 1.6 %cut.1 = (bf16[32,8192]{1,0:T(8,128)(2,1)S(1)}, bf16[32,6144]{1,0:T(8,128)(2,1)S(1)}, bf16[32,8192]{1,0:T(8,128)(2,1)S(1)}, bf16[32,8192]{1,0:T(8,128)(2,1)S(1)}) custom-call(bf16[32,32768]{1,0:T(8,128)(2,1)} %refs_0_.1), custom_call_target="tpu_custom_call" | custom-call | bytes 2097152 | tf_op jit(solution)/shard_map/cut/pallas_call | solution.py:173
  2.3 6.0 %collective-permute-start.3 = (bf16[32,8192]{1,0:T(8,128)(2,1)S(1)}, bf16[32,8192]{1,0:T(8,128)(2,1)S(1)}, u32[]{:S(2)}, u32[]{:S(2)}) collective-permute-start(bf16[32,8192]{1,0:T(8,128)(2,1)S(1)} %get-tuple-element.15), channel_id=1, source_target_pairs={{0,112},{16,0},{32,16},{48,32},{64,48},{80,64},{96,80},{112,96},{1... | collective-permute-start | bytes 1572872 | tf_op jit(solution)/shard_map/ppermute | solution.py:333
  8.3 0.0 collective-permute-start.2
  8.3 0.0 collective-permute-start
  8.3 5.1 %collective-permute-start.1 = (bf16[32,8192]{1,0:T(8,128)(2,1)S(1)}, bf16[32,8192]{1,0:T(8,128)(2,1)S(1)}, u32[]{:S(2)}, u32[]{:S(2)}) collective-permute-start(bf16[32,8192]{1,0:T(8,128)(2,1)S(1)} %get-tuple-element.11), channel_id=1, source_target_pairs={{0,112},{16,0},{32,16},{48,32},{64,48},{80,64},{96,80},{112,96},{1... | collective-permute-start | bytes 1572872 | tf_op jit(solution)/shard_map/ppermute | solution.py:333
  13.4 3.9 %table.1 = (bf16[1024,2048]{1,0:T(8,128)(2,1)S(1)}, bf16[1024,2048]{1,0:T(8,128)(2,1)S(1)}) custom-call(s32[8,128]{1,0:T(8,128)S(1)} %bitcast.2), custom_call_target="tpu_custom_call" | custom-call | flops 33554432 | bytes 8388608 | tf_op jit(solution)/shard_map/table/pallas_call | solution.py:110
  17.3 0.0 copy-start
  17.3 0.0 copy-start.1
  17.4 6.8 %weights.1.refs_6_.weight_ref = bf16[8,2,256,512]{3,2,1,0:T(8,128)(2,1)S(1)} custom-call(s32[1024]{0:T(1024)S(1)} %copy-done.4, s32[256]{0:T(256)S(1)} %copy-done.5, f32[256,512]{1,0:T(8,128)S(1)} %copy-done.2, f32[256,512]{1,0:T(8,128)S(1)} %copy-done.3), custom_call_target="tpu_custom_call" | custom-call | flops 52428800 | bytes 6291456 | tf_op jit(solution)/shard_map/weights/pallas_call | solution.py:148
  24.2 0.0 collective-permute-done.2.refs_1_
  24.2 0.0 collective-permute-done.3.refs_2_
  24.2 6.9 %spectra0.1 = (bf16[128,64,128]{2,1,0:T(8,128)(2,1)S(1)}, f32[256,2048]{1,0:T(8,128)S(1)}) custom-call(bf16[32,32768]{1,0:T(8,128)(2,1)S(1)} %copy-done, bf16[32,6144]{1,0:T(8,128)(2,1)S(1)} %collective-permute-done.2.refs_1_, bf16[32,8192]{1,0:T(8,128)(2,1)S(1)} %collective-permute-done.3.refs_2_, f32[16,2048]{1,0:T(8,128)S(1)} %copy-done.1, ...), custom_call_target="tpu_custom_call" | custom-call | flops 2147483648 | bytes 12582912 | tf_op jit(solution)/shard_map/spectra0/pallas_call | solution.py:251
  31.1 1.7 %collective-permute-done.refs_0_ = bf16[32,8192]{1,0:T(8,128)(2,1)S(1)} collective-permute-done((bf16[32,8192]{1,0:T(8,128)(2,1)S(1)}, bf16[32,8192]{1,0:T(8,128)(2,1)S(1)}, u32[]{:S(2)}, u32[]{:S(2)}) %collective-permute-start) | collective-permute-done | bytes 524320 | tf_op jit(solution)/shard_map/ppermute | solution.py:332
  32.8 0.0 collective-permute-done.1.refs_1_
  32.8 3.1 %spectra1.1 = bf16[128,64,128]{2,1,0:T(8,128)(2,1)S(1)} custom-call(bf16[32,8192]{1,0:T(8,128)(2,1)S(1)} %collective-permute-done.refs_0_, bf16[32,8192]{1,0:T(8,128)(2,1)S(1)} %collective-permute-done.1.refs_1_, f32[16,2048]{1,0:T(8,128)S(1)} %copy-done.1, bf16[1024,2048]{1,0:T(8,128)(2,1)S(1)} %get-tuple-element.12.refs_4_.refs_3_, ...), custom_call_target="tpu_custom_call", output_to_operand_aliasing={{}: (6, {})} | custom-call | flops 2147483648 | bytes 12582912 | tf_op jit(solution)/shard_map/spectra1/pallas_call | solution.py:251
  35.9 0.0 copy-start.6
  35.9 0.0 copy-start.7
  35.9 0.0 copy-start.8
  35.9 0.0 copy-start.9
  35.9 39.4 %all_to_all.5.got_ref = bf16[128,64,128]{2,1,0:T(8,128)(2,1)S(1)} all-to-all(bf16[128,64,128]{2,1,0:T(8,128)(2,1)S(1)} %spectra1.1), channel_id=1, replica_groups=mesh['tm'=8,'freq'=16] {'freq','tm'}, dimensions={0} | all-to-all | bytes 4194304 | tf_op jit(solution)/shard_map/all_to_all | solution.py:343
  75.3 0.0 copy-done.6
  75.3 0.0 copy-done.8
  75.3 6.8 %pairs.1 = (bf16[8,2,512,512]{3,2,1,0:T(8,128)(2,1)}, bf16[8,128,2,256]{3,2,1,0:T(2,128)(2,1)}) custom-call(s32[1,256]{1,0:T(1,128)S(1)} %bitcast.3, bf16[256,512]{1,0:T(8,128)(2,1)S(1)} %copy-done.8, bf16[512,512]{1,0:T(8,128)(2,1)S(1)} %copy-done.7, bf16[256,256]{1,0:T(8,128)(2,1)S(1)} %copy-done.9, bf16[128,64,128]{2,1,0:T(8,128)(2,1)S(1)} %all_to_all.5.got_ref, ...), custom_call_target="tpu_custom_call" | custom-call | flops 5000000000 | bytes 16777216 | tf_op jit(solution)/shard_map/pairs/pallas_call | solution.py:309
  (11 shorter events, 0.0 us)
Async XLA Ops:
  0.6 12.8 %copy-start.4 = (s32[1024]{0:T(1024)S(1)}, s32[1024]{0:T(1024)}, u32[]{:S(2)}) copy-start(s32[1024]{0:T(1024)} %owner_ref.1) | copy-start | bytes 12292
  0.6 16.7 %copy-start.3 = (f32[256,512]{1,0:T(8,128)S(1)}, f32[256,512]{1,0:T(8,128)}, u32[]{:S(2)}) copy-start(f32[256,512]{1,0:T(8,128)} %delays_ref.1) | copy-start | bytes 1572868
  0.7 16.7 %copy-start.2 = (f32[256,512]{1,0:T(8,128)S(1)}, f32[256,512]{1,0:T(8,128)}, u32[]{:S(2)}) copy-start(f32[256,512]{1,0:T(8,128)} %gains_ref.1) | copy-start | bytes 1572868
  0.7 16.7 %copy-start.5 = (s32[256]{0:T(256)S(1)}, s32[256]{0:T(256)}, u32[]{:S(2)}) copy-start(s32[256]{0:T(256)} %beam_ref.1) | copy-start | bytes 3076
  2.3 21.9 %collective-permute-start.3 = (bf16[32,8192]{1,0:T(8,128)(2,1)S(1)}, bf16[32,8192]{1,0:T(8,128)(2,1)S(1)}, u32[]{:S(2)}, u32[]{:S(2)}) collective-permute-start(bf16[32,8192]{1,0:T(8,128)(2,1)S(1)} %get-tuple-element.15), channel_id=1, source_target_pairs={{0,112},{16,0},{32,16},{48,32},{64,48},{80,64},{96,80},{112,96},{1... | collective-permute-start | bytes 1572872 | tf_op jit(solution)/shard_map/ppermute | solution.py:333
  8.3 15.9 %collective-permute-start.2 = (bf16[32,6144]{1,0:T(8,128)(2,1)S(1)}, bf16[32,6144]{1,0:T(8,128)(2,1)S(1)}, u32[]{:S(2)}, u32[]{:S(2)}) collective-permute-start(bf16[32,6144]{1,0:T(8,128)(2,1)S(1)} %get-tuple-element.14), channel_id=1, source_target_pairs={{0,16},{16,32},{32,48},{48,64},{64,80},{80,96},{96,112},{112,0},{1... | collective-permute-start | bytes 1179656 | tf_op jit(solution)/shard_map/ppermute | solution.py:332
  8.3 24.5 %collective-permute-start = (bf16[32,8192]{1,0:T(8,128)(2,1)S(1)}, bf16[32,8192]{1,0:T(8,128)(2,1)S(1)}, u32[]{:S(2)}, u32[]{:S(2)}) collective-permute-start(bf16[32,8192]{1,0:T(8,128)(2,1)S(1)} %get-tuple-element.10), channel_id=1, source_target_pairs={{0,16},{16,32},{32,48},{48,64},{64,80},{80,96},{96,112},{112,0},{1... | collective-permute-start | bytes 1572872 | tf_op jit(solution)/shard_map/ppermute | solution.py:332
  8.3 24.5 %collective-permute-start.1 = (bf16[32,8192]{1,0:T(8,128)(2,1)S(1)}, bf16[32,8192]{1,0:T(8,128)(2,1)S(1)}, u32[]{:S(2)}, u32[]{:S(2)}) collective-permute-start(bf16[32,8192]{1,0:T(8,128)(2,1)S(1)} %get-tuple-element.11), channel_id=1, source_target_pairs={{0,112},{16,0},{32,16},{48,32},{64,48},{80,64},{96,80},{112,96},{1... | collective-permute-start | bytes 1572872 | tf_op jit(solution)/shard_map/ppermute | solution.py:333
  17.3 6.9 %copy-start = (bf16[32,32768]{1,0:T(8,128)(2,1)S(1)}, bf16[32,32768]{1,0:T(8,128)(2,1)}, u32[]{:S(2)}) copy-start(bf16[32,32768]{1,0:T(8,128)(2,1)} %refs_0_.1) | copy-start | bytes 6291460
  17.3 6.9 %copy-start.1 = (f32[16,2048]{1,0:T(8,128)S(1)}, f32[16,2048]{1,0:T(8,128)}, u32[]{:S(2)}) copy-start(f32[16,2048]{1,0:T(8,128)} %constant.8.clone.refs_3_.refs_2_) | copy-start | bytes 393220
  35.9 39.5 %copy-start.6 = (s32[256]{0:T(256)S(1)}, s32[256]{0:T(256)}, u32[]{:S(2)}) copy-start(s32[256]{0:T(256)} %param.11) | copy-start | bytes 3076
  35.9 39.5 %copy-start.7 = (bf16[512,512]{1,0:T(8,128)(2,1)S(1)}, bf16[512,512]{1,0:T(8,128)(2,1)}, u32[]{:S(2)}) copy-start(bf16[512,512]{1,0:T(8,128)(2,1)} %constant.10.clone.lanes_ref) | copy-start | bytes 1572868
  35.9 39.4 %copy-start.8 = (bf16[256,512]{1,0:T(8,128)(2,1)S(1)}, bf16[256,512]{1,0:T(8,128)(2,1)}, u32[]{:S(2)}) copy-start(bf16[256,512]{1,0:T(8,128)(2,1)} %constant.9.clone.twice_ref) | copy-start | bytes 786436
  35.9 39.4 %copy-start.9 = (bf16[256,256]{1,0:T(8,128)(2,1)S(1)}, bf16[256,256]{1,0:T(8,128)(2,1)}, u32[]{:S(2)}) copy-start(bf16[256,256]{1,0:T(8,128)(2,1)} %constant.11.clone.frames_ref) | copy-start | bytes 393220
